TPU v7x, 32 devices: a whole 2x2x4 slice. The times are simulated.
32 devices in a mesh: grp: 2 (over y), wid: 4 (over z), hgt: 4 (over x, core).
Axes of the slice: x: 2, y: 2, z: 4, core: 2. Of those that a mesh axis runs over, the one named last changes fastest.
Arguments:
- latent_query: bfloat16 [8, 16, 32, 1536], P('grp', 'hgt', 'wid'), parts along dimension 0, may hold values from -20 to 20
- latent_key: bfloat16 [8, 16, 32, 1536], P('grp', 'hgt', 'wid'), parts along dimension 0, may hold values from -20 to 20
- latent_value: bfloat16 [8, 16, 32, 1536], P('grp', 'hgt', 'wid'), parts along dimension 0, may hold values from -6 to 6
- latent_grad: bfloat16 [8, 16, 32, 1536], P('grp', 'hgt', 'wid'), parts along dimension 0, may hold values from -6 to 6
- text_query: bfloat16 [256, 1536], P('grp'), parts along dimension 0, may hold values from -20 to 20
- text_key: bfloat16 [256, 1536], P('grp'), parts along dimension 0, may hold values from -20 to 20
- text_value: bfloat16 [256, 1536], P('grp'), parts along dimension 0, may hold values from -6 to 6
- text_grad: bfloat16 [256, 1536], P('grp'), parts along dimension 0, may hold values from -6 to 6
- text_valid: int32 [256], P('grp'), parts along dimension 0, may hold values 0 or 1
- windows: int32 [8, 9], replicated, may hold values from -1 to 7, as said below
Outputs:
- latent_out: bfloat16 [8, 16, 32, 1536], P('grp', 'hgt', 'wid'), parts along dimension 0
- grad_query: bfloat16 [8, 16, 32, 1536], P('grp', 'hgt', 'wid'), parts along dimension 0
- grad_key: bfloat16 [8, 16, 32, 1536], P('grp', 'hgt', 'wid'), parts along dimension 0
- grad_value: bfloat16 [8, 16, 32, 1536], P('grp', 'hgt', 'wid'), parts along dimension 0
- text_out: bfloat16 [256, 1536], P(('grp', 'wid', 'hgt')), parts along dimension 0
- text_grad_query: bfloat16 [256, 1536], P(('grp', 'wid', 'hgt')), parts along dimension 0
- text_grad_key: bfloat16 [256, 1536], P(('grp', 'wid', 'hgt')), parts along dimension 0
- text_grad_value: bfloat16 [256, 1536], P(('grp', 'wid', 'hgt')), parts along dimension 0
There are 2 independent parts, one for each index of `grp`. A program takes and returns all parts, laid end to end along the dimension named above; an argument that names none is the same for every part. Nothing has to cross between parts.
Inputs may be any that keep to these rules, and one draw needn't show every extreme that they name: `windows`: slot s of tile t holds the tile (s // 3 - 1) tile rows and (s % 3 - 1) tile columns away from t, or -1; it holds -1 where that tile lies outside the grid, and slot 4 always holds t. Tiles are numbered row by row, 4 to a row.
All inputs are finite; a program needn't handle non-finite values.
Results may differ from a plain program's by a relative error of at most 0.034.
Values may be sent and summed in bfloat16 or wider, within the bound.
A program may use at most 128 MiB of HBM per device.

v0:
```python
import functools

import jax
import jax.numpy as jnp
from jax import lax
from jax.experimental import pallas as pl
from jax.experimental.pallas import tpu as pltpu
from jax.sharding import PartitionSpec as P

D = 128
SCALE = D ** (-0.5)
NEG = -1e30
F32 = jnp.float32
BF16 = jnp.bfloat16
PARAMS = pltpu.CompilerParams(
    dimension_semantics=("arbitrary",), vmem_limit_bytes=48 * 1024 * 1024
)


def dot_nt(a, b):
    return lax.dot_general(a, b, (((1,), (1,)), ((), ())), preferred_element_type=F32)


def dot_nn(a, b):
    return lax.dot_general(a, b, (((1,), (0,)), ((), ())), preferred_element_type=F32)


def dot_tn(a, b):
    return lax.dot_general(a, b, (((0,), (0,)), ((), ())), preferred_element_type=F32)


def round_bf16(x):
    return x.astype(BF16).astype(F32)


def pack_kernel(par, *refs):
    count = (len(refs) - 2) // 2
    kept, sent = refs[-2:]
    for at in range(count):
        kept[at] = refs[2 * at][...]
        sent[at] = refs[2 * at + 1][...]


def pack_halves(par, arrays):
    rows, channels = arrays[0].shape
    half = channels // 2
    count = len(arrays)
    specs = []
    for _ in arrays:
        specs.append(pl.BlockSpec((rows, half), lambda i, p: (0, p[0])))
        specs.append(pl.BlockSpec((rows, half), lambda i, p: (0, 1 - p[0])))
    out = jax.ShapeDtypeStruct((count, rows, half), BF16)
    return pl.pallas_call(
        pack_kernel,
        grid_spec=pltpu.PrefetchScalarGridSpec(
            num_scalar_prefetch=1,
            grid=(1,),
            in_specs=specs,
            out_specs=[pl.BlockSpec((count, rows, half), lambda i, p: (0, 0, 0))] * 2,
        ),
        out_shape=[out, out],
        compiler_params=PARAMS,
        name="pack_halves",
    )(par, *[a for a in arrays for _ in range(2)])


def text_scores(kv, tq, tg, tk, tv, bias):
    query, grad = tq[...], tg[...]
    near = dot_nt(kv[0], query) * SCALE
    own = dot_nt(tk[...], query) * SCALE + bias[...]
    return near, own, dot_nt(kv[1], grad), dot_nt(tv[...], grad)


def text_stats_kernel(par, kv, tq, tg, tk, tv, bias, stats):
    near, own, dp_near, dp_own = text_scores(kv, tq, tg, tk, tv, bias)
    top = jnp.maximum(
        jnp.max(near, axis=0, keepdims=True), jnp.max(own, axis=0, keepdims=True)
    )
    e_near = jnp.exp(near - top)
    e_own = jnp.exp(own - top)
    total = jnp.sum(e_near, axis=0, keepdims=True) + jnp.sum(e_own, axis=0, keepdims=True)
    mix = jnp.sum(e_near * dp_near, axis=0, keepdims=True) + jnp.sum(
        e_own * dp_own, axis=0, keepdims=True
    )
    stats[0] = jnp.concatenate([top, total, mix, jnp.zeros((5, top.shape[1]), F32)], axis=0)


def text_grads_kernel(par, gathered, kv, tq, tg, tk, tv, bias, rows, self_keys, near_keys):
    near, own, dp_near, dp_own = text_scores(kv, tq, tg, tk, tv, bias)
    parts = gathered[:, 0, 0]
    tops = parts[:, 0, :]
    top = jnp.max(tops, axis=0, keepdims=True)
    factor = jnp.exp(tops - top)
    total = jnp.sum(parts[:, 1, :] * factor, axis=0, keepdims=True)
    delta = jnp.sum(parts[:, 2, :] * factor, axis=0, keepdims=True) / total
    lse = top + jnp.log(total)
    p_near = jnp.exp(near - lse)
    p_own = jnp.exp(own - lse)
    low_near = p_near.astype(BF16)
    low_own = p_own.astype(BF16)
    ds_near = (p_near * (dp_near - delta)).astype(BF16)
    ds_own = (p_own * (dp_own - delta)).astype(BF16)
    query, grad = tq[...], tg[...]
    rows[0] = (dot_tn(low_near, kv[1]) + dot_tn(low_own, tv[...])).astype(BF16)
    rows[1] = (dot_tn(ds_near, kv[0]) + dot_tn(ds_own, tk[...])).astype(BF16)
    self_keys[0] = dot_nn(ds_own, query)
    self_keys[1] = dot_nn(low_own, grad)
    near_keys[0] = dot_nn(ds_near, query)
    near_keys[1] = dot_nn(low_near, grad)


def query_kernel(count, par, gates, qg, *refs):
    tiles = refs[:count]
    tk, tv, bias, self_keys, kept, sent, stats, text_rows, score = refs[count:]
    half = qg.shape[1] // 2
    query, grad = qg[0], qg[1]
    size = qg.shape[1]
    text = tk.shape[0]
    top = None
    for at in range(count):
        part = dot_nt(tiles[at][0], query) * SCALE + gates[at]
        score[at * size : (at + 1) * size] = part
        peak = jnp.max(part, axis=0, keepdims=True)
        top = peak if top is None else jnp.maximum(top, peak)
    part = dot_nt(tk[...], query) * SCALE + bias[...][:, :1]
    score[count * size : count * size + text] = part
    shift = round_bf16(jnp.maximum(top, jnp.max(part, axis=0, keepdims=True)))
    spans = [(at * size, size) for at in range(count)] + [(count * size, text)]
    total = jnp.zeros_like(shift)
    for first, length in spans:
        weight = jnp.exp(score[first : first + length] - shift)
        score[first : first + length] = weight
        total = total + jnp.sum(weight, axis=0, keepdims=True)
    inverse = round_bf16(1.0 / total)
    keys = [(lambda at=at: tiles[at][0]) for at in range(count)] + [lambda: tk[...]]
    values = [(lambda at=at: tiles[at][1]) for at in range(count)] + [lambda: tv[...]]
    out = jnp.zeros((D, size), F32)
    for at, (first, length) in enumerate(spans):
        low = (score[first : first + length] * inverse).astype(BF16)
        out = out + dot_tn(values[at](), low)
        if at == count:
            text_rows[1] = (self_keys[1] + dot_nn(low, grad)).astype(BF16)
    out = round_bf16(out)
    grad_t = grad.astype(F32).T
    delta = round_bf16(jnp.sum(grad_t * out, axis=0, keepdims=True))
    query_grad = jnp.zeros((D, size), F32)
    for at, (first, length) in enumerate(spans):
        dp = dot_nt(values[at](), grad)
        ds = (score[first : first + length] * inverse * (dp - delta)).astype(BF16)
        query_grad = query_grad + dot_tn(keys[at](), ds)
        if at == count:
            text_rows[0] = (self_keys[0] + dot_nn(ds, query)).astype(BF16)
    out = out.T.astype(BF16)
    query_grad = (query_grad * SCALE).T.astype(BF16)
    kept[0] = out[:half]
    kept[1] = query_grad[:half]
    sent[0] = out[half:]
    sent[1] = query_grad[half:]
    stats[0] = jnp.concatenate([shift, inverse, delta, jnp.zeros((5, size), F32)], axis=0)


def key_kernel(count, gates, kv, near_keys, *refs):
    tiles = refs[:count]
    stats = refs[count : 2 * count]
    kept, sent = refs[2 * count :]
    half = kv.shape[1] // 2
    key, value = kv[0], kv[1]
    key_grad = near_keys[0]
    value_grad = near_keys[1]
    for at in range(count):
        query, grad = tiles[at][0], tiles[at][1]
        shift, inverse, delta = (stats[at][0, row : row + 1, :] for row in range(3))
        prob = jnp.exp(dot_nt(key, query) * SCALE + (gates[at] - shift)) * inverse
        ds = (prob * (dot_nt(value, grad) - delta)).astype(BF16)
        value_grad = value_grad + dot_nn(prob.astype(BF16), grad)
        key_grad = key_grad + dot_nn(ds, query)
    key_grad = (key_grad * SCALE).astype(BF16)
    value_grad = value_grad.astype(BF16)
    kept[0] = key_grad[:half]
    kept[1] = value_grad[:half]
    sent[0] = key_grad[half:]
    sent[1] = value_grad[half:]


def shifted(value, axis, steps):
    count = lax.axis_size(axis)
    pairs = [(at, at + steps) for at in range(count) if 0 <= at + steps < count]
    return lax.ppermute(value, axis, pairs)


def swapped(value, stride):
    count = lax.axis_size("hgt")
    return lax.ppermute(value, "hgt", [(at, at ^ stride) for at in range(count)])


def fetch(value):
    if lax.axis_size("hgt") == 4:
        columns = [value, swapped(value, 2)]
    else:
        columns = [value, shifted(value, "hgt", 2), shifted(value, "hgt", -2)]
    return [
        part
        for column in columns
        for part in (column, shifted(column, "wid", 1), shifted(column, "wid", -1))
    ]


def halves_back(parity, mine, theirs):
    return jnp.where(
        parity == 0,
        jnp.concatenate([mine, theirs], axis=-1),
        jnp.concatenate([theirs, mine], axis=-1),
    )


def per_device(
    latent_query,
    latent_key,
    latent_value,
    latent_grad,
    text_query,
    text_key,
    text_value,
    text_grad,
    text_valid,
    windows,
):
    block = latent_query.shape
    channels = block[3]
    rows = block[0] * block[1] * block[2]
    size = 2 * rows
    width = channels // 2
    heads = width // D
    text = text_query.shape[0]
    wid_size, hgt_size = lax.axis_size("wid"), lax.axis_size("hgt")
    devices = wid_size * hgt_size
    wid_at, hgt_at = lax.axis_index("wid"), lax.axis_index("hgt")
    parity = hgt_at % 2
    tile_row, tile_rows = hgt_at // 2, hgt_size // 2
    tile_here = tile_row * wid_size + wid_at
    par = parity.astype(jnp.int32).reshape(1)

    row_steps = [0, 1 - 2 * tile_row] if hgt_size == 4 else [0, -1, 1]
    sees, seen = [], []
    for dr in row_steps:
        for dc in (0, -1, 1):
            row, col = tile_row + dr, wid_at + dc
            inside = (row >= 0) & (row < tile_rows) & (col >= 0) & (col < wid_size)
            other = jnp.clip(row, 0, tile_rows - 1) * wid_size + jnp.clip(col, 0, wid_size - 1)
            slot = (dr + 1) * 3 + dc + 1
            sees.append(inside & (windows[tile_here, slot] >= 0))
            seen.append(inside & (windows[other, 8 - slot] >= 0))
    count = len(sees)
    gate_query = jnp.where(jnp.stack(sees), 0.0, NEG).astype(F32)
    gate_key = jnp.where(jnp.stack(seen), 0.0, NEG).astype(F32)
    text_bias = jnp.broadcast_to(jnp.where(text_valid == 1, 0.0, NEG).astype(F32)[:, None], (text, text))
    self_bias = jnp.where(tile_here == 0, text_bias, NEG)

    flat = [a.reshape(rows, channels) for a in (latent_key, latent_value, latent_query, latent_grad)]
    kv_kept, kv_sent = pack_halves(par, flat[:2])
    qg_kept, qg_sent = pack_halves(par, flat[2:])
    kv = jnp.concatenate([kv_kept, swapped(kv_sent, 1)], axis=1)
    qg = jnp.concatenate([qg_kept, swapped(qg_sent, 1)], axis=1)
    kv_tiles = fetch(kv)
    qg_tiles = fetch(qg)

    tile_spec = pl.BlockSpec((2, size, D), lambda h, *_: (0, 0, h))
    text_spec = pl.BlockSpec((text, D), lambda h, p, *_: (0, p[0] * heads + h))
    bias_spec = pl.BlockSpec((text, text), lambda h, *_: (0, 0))
    row_spec = pl.BlockSpec((2, text, D), lambda h, *_: (0, 0, h))
    half_spec = pl.BlockSpec((2, rows, D), lambda h, *_: (0, 0, h))
    stat_spec = pl.BlockSpec((1, 8, size), lambda h, *_: (h, 0, 0))
    smem = pl.BlockSpec(memory_space=pltpu.SMEM)

    text_stats = pl.pallas_call(
        text_stats_kernel,
        grid_spec=pltpu.PrefetchScalarGridSpec(
            num_scalar_prefetch=1,
            grid=(heads,),
            in_specs=[tile_spec] + [text_spec] * 4 + [bias_spec],
            out_specs=pl.BlockSpec((1, 8, text), lambda h, p: (h, 0, 0)),
        ),
        out_shape=jax.ShapeDtypeStruct((heads, 8, text), F32),
        compiler_params=PARAMS,
        cost_estimate=pl.CostEstimate(
            flops=4 * heads * (size + text) * text * D, bytes_accessed=4 * size * width, transcendentals=0
        ),
        name="text_stats",
    )(par, kv, text_query, text_grad, text_key, text_value, self_bias)
    gathered = lax.all_gather(text_stats, ("wid", "hgt")).reshape(devices // 2, 2, heads, 8, text)

    text_rows, self_keys, near_keys = pl.pallas_call(
        text_grads_kernel,
        grid_spec=pltpu.PrefetchScalarGridSpec(
            num_scalar_prefetch=1,
            grid=(heads,),
            in_specs=[
                pl.BlockSpec((devices // 2, 1, 1, 8, text), lambda h, p: (0, p[0], h, 0, 0)),
                tile_spec,
            ]
            + [text_spec] * 4
            + [bias_spec],
            out_specs=[row_spec, row_spec, tile_spec],
        ),
        out_shape=[
            jax.ShapeDtypeStruct((2, text, width), BF16),
            jax.ShapeDtypeStruct((2, text, width), F32),
            jax.ShapeDtypeStruct((2, size, width), F32),
        ],
        compiler_params=PARAMS,
        cost_estimate=pl.CostEstimate(
            flops=12 * heads * (size + text) * text * D, bytes_accessed=8 * size * width, transcendentals=0
        ),
        name="text_grads",
    )(par, gathered, kv, text_query, text_grad, text_key, text_value, self_bias)

    work = heads * size * (count * size + text) * D
    half_shape = jax.ShapeDtypeStruct((2, rows, width), BF16)
    query_kept, query_sent, stats, key_rows = pl.pallas_call(
        functools.partial(query_kernel, count),
        grid_spec=pltpu.PrefetchScalarGridSpec(
            num_scalar_prefetch=1,
            grid=(heads,),
            in_specs=[smem, tile_spec]
            + [tile_spec] * count
            + [text_spec, text_spec, bias_spec, row_spec],
            out_specs=[half_spec, half_spec, stat_spec, row_spec],
            scratch_shapes=[pltpu.VMEM((count * size + text, size), F32)],
        ),
        out_shape=[
            half_shape,
            half_shape,
            jax.ShapeDtypeStruct((heads, 8, size), F32),
            jax.ShapeDtypeStruct((2, text, width), BF16),
        ],
        compiler_params=PARAMS,
        cost_estimate=pl.CostEstimate(
            flops=8 * work, bytes_accessed=4 * size * width * (count + 2), transcendentals=work // D
        ),
        name="query_side",
    )(par, gate_query, qg, *kv_tiles, text_key, text_value, text_bias, self_keys)

    stat_tiles = fetch(stats)
    query_back = swapped(query_sent, 1)
    packed = jnp.concatenate([text_rows, key_rows], axis=0)
    owned = text // devices
    packed = packed.reshape(4, devices, owned, width)
    landed = lax.all_to_all(packed, ("wid", "hgt"), 1, 1)

    key_kept, key_sent = pl.pallas_call(
        functools.partial(key_kernel, count),
        grid_spec=pltpu.PrefetchScalarGridSpec(
            num_scalar_prefetch=1,
            grid=(heads,),
            in_specs=[tile_spec, tile_spec] + [tile_spec] * count + [stat_spec] * count,
            out_specs=[half_spec, half_spec],
        ),
        out_shape=[half_shape, half_shape],
        compiler_params=PARAMS,
        cost_estimate=pl.CostEstimate(
            flops=8 * work, bytes_accessed=4 * size * width * (count + 2), transcendentals=work // D
        ),
        name="key_side",
    )(gate_key, kv, near_keys, *qg_tiles, *stat_tiles)
    key_back = swapped(key_sent, 1)

    latent = [
        halves_back(parity, mine[at], theirs[at]).reshape(block)
        for mine, theirs in ((query_kept, query_back), (key_kept, key_back))
        for at in range(2)
    ]
    summed = jnp.sum(landed.reshape(4, devices // 2, 2, owned, width).astype(F32), axis=1)
    summed = jnp.swapaxes(summed, 1, 2).reshape(4, owned, channels)
    text_outs = [
        summed[0].astype(BF16),
        (summed[1] * SCALE).astype(BF16),
        (summed[2] * SCALE).astype(BF16),
        summed[3].astype(BF16),
    ]
    return tuple(latent + text_outs)


def solution(mesh):
    tiles = P("grp", "hgt", "wid", None)
    rows = P(("grp", "wid", "hgt"), None)
    return jax.shard_map(
        per_device,
        mesh=mesh,
        in_specs=(tiles,) * 4 + (P("grp", None),) * 4 + (P("grp"), P()),
        out_specs=(tiles,) * 4 + (rows,) * 4,
        check_vma=False,
    )
```

profile of v0, /device:TPU:9, one launch (start us, length us, event | category | flops | bytes accessed | tf_op | source)
XLA Modules:
  0.0 166.8 jit_solution(2632382400874541985)
XLA Ops:
  3.5 1.3 collective-permute-done.1
  7.0 3.2 %collective-permute-start.2 = (bf16[2,256,768]{2,1,0:T(8,128)(2,1)S(1)}, bf16[2,256,768]{2,1,0:T(8,128)(2,1)}, u32[]{:S(2)}, u32[]{:S(2)}) collective-permute-start(bf16[2,256,768]{2,1,0:T(8,128)(2,1)S(1)} %constant_dynamic-update-slice_fusion.2.kv.refs_0_), channel_id=1, source_target_pairs={{0,4},{4,8},{8,12},{1,5},{5,9},{9,13},{2,6},{6,10},{10,14},{3,7},{... | collective-permute-start | bytes 2359304 | tf_op jit(solution)/shard_map/ppermute | solution.py:188
  10.2 3.0 %collective-permute-start.3 = (bf16[2,256,768]{2,1,0:T(8,128)(2,1)S(1)}, bf16[2,256,768]{2,1,0:T(8,128)(2,1)}, u32[]{:S(2)}, u32[]{:S(2)}) collective-permute-start(bf16[2,256,768]{2,1,0:T(8,128)(2,1)S(1)} %constant_dynamic-update-slice_fusion.2.kv.refs_0_), channel_id=1, source_target_pairs={{4,0},{8,4},{12,8},{5,1},{9,5},{13,9},{6,2},{10,6},{14,10},{7,3},{... | collective-permute-start | bytes 2359304 | tf_op jit(solution)/shard_map/ppermute | solution.py:188
  13.5 10.2 %collective-permute-done.4.refs_3_ = bf16[2,256,768]{2,1,0:T(8,128)(2,1)} collective-permute-done((bf16[2,256,768]{2,1,0:T(8,128)(2,1)S(1)}, bf16[2,256,768]{2,1,0:T(8,128)(2,1)}, u32[]{:S(2)}, u32[]{:S(2)}) %collective-permute-start.4) | collective-permute-done | bytes 786464 | tf_op jit(solution)/shard_map/ppermute | solution.py:193
  23.7 3.2 %collective-permute-start.5 = (bf16[2,256,768]{2,1,0:T(8,128)(2,1)}, bf16[2,256,768]{2,1,0:T(8,128)(2,1)}, u32[]{:S(2)}, u32[]{:S(2)}) collective-permute-start(bf16[2,256,768]{2,1,0:T(8,128)(2,1)} %collective-permute-done.4.refs_3_), channel_id=1, source_target_pairs={{0,4},{4,8},{8,12},{1,5},{5,9},{9,13},{2,6},{6,10},{10,14},{3,7},{... | collective-permute-start | bytes 2359304 | tf_op jit(solution)/shard_map/ppermute | solution.py:188
  31.7 2.8 %collective-permute-start.6 = (bf16[2,256,768]{2,1,0:T(8,128)(2,1)}, bf16[2,256,768]{2,1,0:T(8,128)(2,1)}, u32[]{:S(2)}, u32[]{:S(2)}) collective-permute-start(bf16[2,256,768]{2,1,0:T(8,128)(2,1)} %collective-permute-done.4.refs_3_), channel_id=1, source_target_pairs={{4,0},{8,4},{12,8},{5,1},{9,5},{13,9},{6,2},{10,6},{14,10},{7,3},{... | collective-permute-start | bytes 2359304 | tf_op jit(solution)/shard_map/ppermute | solution.py:188
  38.6 2.4 %collective-permute-start.8 = (bf16[2,256,768]{2,1,0:T(8,128)(2,1)S(1)}, bf16[2,256,768]{2,1,0:T(8,128)(2,1)}, u32[]{:S(2)}, u32[]{:S(2)}) collective-permute-start(bf16[2,256,768]{2,1,0:T(8,128)(2,1)S(1)} %constant_dynamic-update-slice_fusion.qg.refs_0_), channel_id=1, source_target_pairs={{0,4},{4,8},{8,12},{1,5},{5,9},{9,13},{2,6},{6,10},{10,14},{3,7},{... | collective-permute-start | bytes 2359304 | tf_op jit(solution)/shard_map/ppermute | solution.py:188
  41.1 3.7 %collective-permute-start.9 = (bf16[2,256,768]{2,1,0:T(8,128)(2,1)S(1)}, bf16[2,256,768]{2,1,0:T(8,128)(2,1)}, u32[]{:S(2)}, u32[]{:S(2)}) collective-permute-start(bf16[2,256,768]{2,1,0:T(8,128)(2,1)S(1)} %constant_dynamic-update-slice_fusion.qg.refs_0_), channel_id=1, source_target_pairs={{4,0},{8,4},{12,8},{5,1},{9,5},{13,9},{6,2},{10,6},{14,10},{7,3},{... | collective-permute-start | bytes 2359304 | tf_op jit(solution)/shard_map/ppermute | solution.py:188
  44.8 2.3 %collective-permute-start.11 = (bf16[2,256,768]{2,1,0:T(8,128)(2,1)}, bf16[2,256,768]{2,1,0:T(8,128)(2,1)}, u32[]{:S(2)}, u32[]{:S(2)}) collective-permute-start(bf16[2,256,768]{2,1,0:T(8,128)(2,1)} %collective-permute-done.10.refs_3_), channel_id=1, source_target_pairs={{0,4},{4,8},{8,12},{1,5},{5,9},{9,13},{2,6},{6,10},{10,14},{3,7},{... | collective-permute-start | bytes 2359304 | tf_op jit(solution)/shard_map/ppermute | solution.py:188
  47.2 2.2 %text_stats.1 = f32[6,8,128]{2,1,0:T(8,128)S(1)} custom-call(s32[1]{0:T(128)} %bitcast.par, bf16[2,256,768]{2,1,0:T(8,128)(2,1)S(1)} %constant_dynamic-update-slice_fusion.2.kv.refs_0_, bf16[128,1536]{1,0:T(8,128)(2,1)S(1)} %copy-done.4, bf16[128,1536]{1,0:T(8,128)(2,1)S(1)} %copy-done.5, bf16[128,1536]{1,0:T(8,128)(2,1)S(1)} %copy-done.6, ...), custom_call_target="tpu_custom_call" | custom-call | flops 150994944 | bytes 786432 | tf_op jit(solution)/shard_map/text_stats/pallas_call | solution.py:275
  49.4 3.9 %collective-permute-start.12 = (bf16[2,256,768]{2,1,0:T(8,128)(2,1)}, bf16[2,256,768]{2,1,0:T(8,128)(2,1)}, u32[]{:S(2)}, u32[]{:S(2)}) collective-permute-start(bf16[2,256,768]{2,1,0:T(8,128)(2,1)} %collective-permute-done.10.refs_3_), channel_id=1, source_target_pairs={{4,0},{8,4},{12,8},{5,1},{9,5},{13,9},{6,2},{10,6},{14,10},{7,3},{... | collective-permute-start | bytes 2359304 | tf_op jit(solution)/shard_map/ppermute | solution.py:188
  53.4 46.1 %all-gather = f32[96,8,128]{2,1,0:T(8,128)S(1)} all-gather(f32[6,8,128]{2,1,0:T(8,128)S(1)} %text_stats.1), channel_id=2, replica_groups=mesh['grp'=2,'wid'=4,'hgt'=4] {'wid','hgt'}, dimensions={0}, use_global_device_ids=true | all-gather | bytes 417792 | tf_op jit(solution)/shard_map/all_gather | solution.py:290
  99.5 3.8 %text_grads.1 = (bf16[2,128,768]{2,1,0:T(8,128)(2,1)S(1)}, f32[2,128,768]{2,1,0:T(8,128)S(1)}, f32[2,256,768]{2,1,0:T(8,128)S(1)}) custom-call(s32[1]{0:T(128)} %bitcast.par, f32[8,2,6,8,128]{4,3,2,1,0:T(8,128)S(1)} %bitcast.48, bf16[2,256,768]{2,1,0:T(8,128)(2,1)S(1)} %constant_dynamic-update-slice_fusion.2.kv.refs_0_, bf16[128,1536]{1,0:T(8,128)(2,1)S(1)} %copy-done.4, ...), custom_call_target="tpu_custom_call" | custom-call | flops 452984832 | bytes 1572864 | tf_op jit(solution)/shard_map/text_grads/pallas_call | solution.py:292
  105.5 13.1 %query_side.1 = (bf16[2,128,768]{2,1,0:T(8,128)(2,1)S(1)}, bf16[2,128,768]{2,1,0:T(8,128)(2,1)S(1)}, f32[6,8,256]{2,1,0:T(8,128)S(1)}, bf16[2,128,768]{2,1,0:T(8,128)(2,1)S(1)}) custom-call(s32[1]{0:T(128)} %bitcast.par, f32[6]{0:T(128)S(1)} %broadcast_select_fusion.2.gates, bf16[2,256,768]{2,1,0:T(8,128)(2,1)S(1)} %constant_dynamic-update-slice_fusion.qg.refs_0_, ...), custom_call_target="tpu_custom_call" | custom-call | flops 2617245696 | bytes 6291456 | tf_op jit(solution)/shard_map/query_side/pallas_call | solution.py:319
  118.6 1.5 collective-permute-start.15
  121.2 7.4 %all-to-all-start = ((bf16[4,16,8,768]{3,2,0,1:T(8,128)(2,1)}), bf16[4,16,8,768]{3,2,0,1:T(8,128)(2,1)}, u32[]{:S(2)}, u32[]{:S(2)}) async-start(bf16[4,16,8,768]{3,2,0,1:T(8,128)(2,1)} %copy.19), calls=%async_computation | async-start | bytes 1572864 | tf_op jit(solution)/shard_map/all_to_all | solution.py:348
  128.5 3.1 %collective-permute-start.13 = (f32[6,8,256]{2,1,0:T(8,128)S(1)}, f32[6,8,256]{2,1,0:T(8,128)S(1)}, u32[]{:S(2)}, u32[]{:S(2)}) collective-permute-start(f32[6,8,256]{2,1,0:T(8,128)S(1)} %get-tuple-element.29.refs_6_), channel_id=1, source_target_pairs={{0,4},{4,8},{8,12},{1,5},{5,9},{9,13},{2,6},{6,10},{10,14},{3,7},{... | collective-permute-start | bytes 147464 | tf_op jit(solution)/shard_map/ppermute | solution.py:188
  131.7 2.2 %collective-permute-start.14 = (f32[6,8,256]{2,1,0:T(8,128)S(1)}, f32[6,8,256]{2,1,0:T(8,128)S(1)}, u32[]{:S(2)}, u32[]{:S(2)}) collective-permute-start(f32[6,8,256]{2,1,0:T(8,128)S(1)} %get-tuple-element.29.refs_6_), channel_id=1, source_target_pairs={{4,0},{8,4},{12,8},{5,1},{9,5},{13,9},{6,2},{10,6},{14,10},{7,3},{... | collective-permute-start | bytes 147464 | tf_op jit(solution)/shard_map/ppermute | solution.py:188
  133.9 3.1 %collective-permute-start.16 = (f32[6,8,256]{2,1,0:T(8,128)S(1)}, f32[6,8,256]{2,1,0:T(8,128)S(1)}, u32[]{:S(2)}, u32[]{:S(2)}) collective-permute-start(f32[6,8,256]{2,1,0:T(8,128)S(1)} %collective-permute-done.15.refs_9_), channel_id=1, source_target_pairs={{0,4},{4,8},{8,12},{1,5},{5,9},{9,13},{2,6},{6,10},{10,14},{3,7},{... | collective-permute-start | bytes 147464 | tf_op jit(solution)/shard_map/ppermute | solution.py:188
  137.0 2.2 %collective-permute-start.17 = (f32[6,8,256]{2,1,0:T(8,128)S(1)}, f32[6,8,256]{2,1,0:T(8,128)S(1)}, u32[]{:S(2)}, u32[]{:S(2)}) collective-permute-start(f32[6,8,256]{2,1,0:T(8,128)S(1)} %collective-permute-done.15.refs_9_), channel_id=1, source_target_pairs={{4,0},{8,4},{12,8},{5,1},{9,5},{13,9},{6,2},{10,6},{14,10},{7,3},{... | collective-permute-start | bytes 147464 | tf_op jit(solution)/shard_map/ppermute | solution.py:188
  139.2 1.5 collective-permute-start.7
  140.8 6.0 %collective-permute-done.13.refs_7_ = f32[6,8,256]{2,1,0:T(8,128)S(1)} collective-permute-done((f32[6,8,256]{2,1,0:T(8,128)S(1)}, f32[6,8,256]{2,1,0:T(8,128)S(1)}, u32[]{:S(2)}, u32[]{:S(2)}) %collective-permute-start.13) | collective-permute-done | bytes 49184 | tf_op jit(solution)/shard_map/ppermute | solution.py:188
  146.7 1.9 %collective-permute-done.14.refs_8_ = f32[6,8,256]{2,1,0:T(8,128)S(1)} collective-permute-done((f32[6,8,256]{2,1,0:T(8,128)S(1)}, f32[6,8,256]{2,1,0:T(8,128)S(1)}, u32[]{:S(2)}, u32[]{:S(2)}) %collective-permute-start.14) | collective-permute-done | bytes 49184 | tf_op jit(solution)/shard_map/ppermute | solution.py:188
  149.7 11.2 %key_side.1 = (bf16[2,128,768]{2,1,0:T(8,128)(2,1)S(1)}, bf16[2,128,768]{2,1,0:T(8,128)(2,1)S(1)}) custom-call(f32[6]{0:T(128)S(1)} %broadcast_select_fusion.1.gates, bf16[2,256,768]{2,1,0:T(8,128)(2,1)S(1)} %constant_dynamic-update-slice_fusion.2.kv.refs_0_, f32[2,256,768]{2,1,0:T(8,128)} %copy-done.8, ...), custom_call_target="tpu_custom_call" | custom-call | flops 2617245696 | bytes 6291456 | tf_op jit(solution)/shard_map/key_side/pallas_call | solution.py:350
  (71 shorter events, 16.5 us)
Async XLA Ops:
  2.7 2.1 %collective-permute-start.1 = (bf16[2,128,768]{2,1,0:T(8,128)(2,1)S(1)}, bf16[2,128,768]{2,1,0:T(8,128)(2,1)S(1)}, u32[]{:S(2)}, u32[]{:S(2)}) collective-permute-start(bf16[2,128,768]{2,1,0:T(8,128)(2,1)S(1)} %get-tuple-element.24), channel_id=1, source_target_pairs={{0,1},{1,0},{2,3},{3,2},{4,5},{5,4},{6,7},{7,6},{8,9},{9,8},{10,11... | collective-permute-start | bytes 1179656 | tf_op jit(solution)/shard_map/ppermute | solution.py:193
  4.8 18.9 %collective-permute-start.4 = (bf16[2,256,768]{2,1,0:T(8,128)(2,1)S(1)}, bf16[2,256,768]{2,1,0:T(8,128)(2,1)}, u32[]{:S(2)}, u32[]{:S(2)}) collective-permute-start(bf16[2,256,768]{2,1,0:T(8,128)(2,1)S(1)} %constant_dynamic-update-slice_fusion.2.kv.refs_0_), channel_id=1, source_target_pairs={{0,2},{1,3},{2,0},{3,1},{4,6},{5,7},{6,4},{7,5},{8,10},{9,11},{10,... | collective-permute-start | bytes 2359304 | tf_op jit(solution)/shard_map/ppermute | solution.py:193
  6.1 41.1 %copy-start.4 = (bf16[128,1536]{1,0:T(8,128)(2,1)S(1)}, bf16[128,1536]{1,0:T(8,128)(2,1)}, u32[]{:S(2)}) copy-start(bf16[128,1536]{1,0:T(8,128)(2,1)} %tq.3) | copy-start | bytes 1179652
  6.1 41.1 %copy-start.5 = (bf16[128,1536]{1,0:T(8,128)(2,1)S(1)}, bf16[128,1536]{1,0:T(8,128)(2,1)}, u32[]{:S(2)}) copy-start(bf16[128,1536]{1,0:T(8,128)(2,1)} %tg.3) | copy-start | bytes 1179652
  6.1 41.1 %copy-start.6 = (bf16[128,1536]{1,0:T(8,128)(2,1)S(1)}, bf16[128,1536]{1,0:T(8,128)(2,1)}, u32[]{:S(2)}) copy-start(bf16[128,1536]{1,0:T(8,128)(2,1)} %refs_6_.1) | copy-start | bytes 1179652
  6.1 41.1 %copy-start.7 = (bf16[128,1536]{1,0:T(8,128)(2,1)S(1)}, bf16[128,1536]{1,0:T(8,128)(2,1)}, u32[]{:S(2)}) copy-start(bf16[128,1536]{1,0:T(8,128)(2,1)} %refs_7_.1) | copy-start | bytes 1179652
  6.2 6.9 %collective-permute-start = (bf16[2,128,768]{2,1,0:T(8,128)(2,1)S(1)}, bf16[2,128,768]{2,1,0:T(8,128)(2,1)S(1)}, u32[]{:S(2)}, u32[]{:S(2)}) collective-permute-start(bf16[2,128,768]{2,1,0:T(8,128)(2,1)S(1)} %get-tuple-element.22), channel_id=1, source_target_pairs={{0,1},{1,0},{2,3},{3,2},{4,5},{5,4},{6,7},{7,6},{8,9},{9,8},{10,11... | collective-permute-start | bytes 1179656 | tf_op jit(solution)/shard_map/ppermute | solution.py:193
  7.0 31.6 %collective-permute-start.2 = (bf16[2,256,768]{2,1,0:T(8,128)(2,1)S(1)}, bf16[2,256,768]{2,1,0:T(8,128)(2,1)}, u32[]{:S(2)}, u32[]{:S(2)}) collective-permute-start(bf16[2,256,768]{2,1,0:T(8,128)(2,1)S(1)} %constant_dynamic-update-slice_fusion.2.kv.refs_0_), channel_id=1, source_target_pairs={{0,4},{4,8},{8,12},{1,5},{5,9},{9,13},{2,6},{6,10},{10,14},{3,7},{... | collective-permute-start | bytes 2359304 | tf_op jit(solution)/shard_map/ppermute | solution.py:188
  10.2 30.9 %collective-permute-start.3 = (bf16[2,256,768]{2,1,0:T(8,128)(2,1)S(1)}, bf16[2,256,768]{2,1,0:T(8,128)(2,1)}, u32[]{:S(2)}, u32[]{:S(2)}) collective-permute-start(bf16[2,256,768]{2,1,0:T(8,128)(2,1)S(1)} %constant_dynamic-update-slice_fusion.2.kv.refs_0_), channel_id=1, source_target_pairs={{4,0},{8,4},{12,8},{5,1},{9,5},{13,9},{6,2},{10,6},{14,10},{7,3},{... | collective-permute-start | bytes 2359304 | tf_op jit(solution)/shard_map/ppermute | solution.py:188
  13.2 31.6 %collective-permute-start.10 = (bf16[2,256,768]{2,1,0:T(8,128)(2,1)S(1)}, bf16[2,256,768]{2,1,0:T(8,128)(2,1)}, u32[]{:S(2)}, u32[]{:S(2)}) collective-permute-start(bf16[2,256,768]{2,1,0:T(8,128)(2,1)S(1)} %constant_dynamic-update-slice_fusion.qg.refs_0_), channel_id=1, source_target_pairs={{0,2},{1,3},{2,0},{3,1},{4,6},{5,7},{6,4},{7,5},{8,10},{9,11},{10,... | collective-permute-start | bytes 2359304 | tf_op jit(solution)/shard_map/ppermute | solution.py:193
  23.7 25.7 %collective-permute-start.5 = (bf16[2,256,768]{2,1,0:T(8,128)(2,1)}, bf16[2,256,768]{2,1,0:T(8,128)(2,1)}, u32[]{:S(2)}, u32[]{:S(2)}) collective-permute-start(bf16[2,256,768]{2,1,0:T(8,128)(2,1)} %collective-permute-done.4.refs_3_), channel_id=1, source_target_pairs={{0,4},{4,8},{8,12},{1,5},{5,9},{9,13},{2,6},{6,10},{10,14},{3,7},{... | collective-permute-start | bytes 2359304 | tf_op jit(solution)/shard_map/ppermute | solution.py:188
  31.7 73.7 %collective-permute-start.6 = (bf16[2,256,768]{2,1,0:T(8,128)(2,1)}, bf16[2,256,768]{2,1,0:T(8,128)(2,1)}, u32[]{:S(2)}, u32[]{:S(2)}) collective-permute-start(bf16[2,256,768]{2,1,0:T(8,128)(2,1)} %collective-permute-done.4.refs_3_), channel_id=1, source_target_pairs={{4,0},{8,4},{12,8},{5,1},{9,5},{13,9},{6,2},{10,6},{14,10},{7,3},{... | collective-permute-start | bytes 2359304 | tf_op jit(solution)/shard_map/ppermute | solution.py:188
  38.6 89.9 %collective-permute-start.8 = (bf16[2,256,768]{2,1,0:T(8,128)(2,1)S(1)}, bf16[2,256,768]{2,1,0:T(8,128)(2,1)}, u32[]{:S(2)}, u32[]{:S(2)}) collective-permute-start(bf16[2,256,768]{2,1,0:T(8,128)(2,1)S(1)} %constant_dynamic-update-slice_fusion.qg.refs_0_), channel_id=1, source_target_pairs={{0,4},{4,8},{8,12},{1,5},{5,9},{9,13},{2,6},{6,10},{10,14},{3,7},{... | collective-permute-start | bytes 2359304 | tf_op jit(solution)/shard_map/ppermute | solution.py:188
  41.1 90.6 %collective-permute-start.9 = (bf16[2,256,768]{2,1,0:T(8,128)(2,1)S(1)}, bf16[2,256,768]{2,1,0:T(8,128)(2,1)}, u32[]{:S(2)}, u32[]{:S(2)}) collective-permute-start(bf16[2,256,768]{2,1,0:T(8,128)(2,1)S(1)} %constant_dynamic-update-slice_fusion.qg.refs_0_), channel_id=1, source_target_pairs={{4,0},{8,4},{12,8},{5,1},{9,5},{13,9},{6,2},{10,6},{14,10},{7,3},{... | collective-permute-start | bytes 2359304 | tf_op jit(solution)/shard_map/ppermute | solution.py:188
  44.8 92.2 %collective-permute-start.11 = (bf16[2,256,768]{2,1,0:T(8,128)(2,1)}, bf16[2,256,768]{2,1,0:T(8,128)(2,1)}, u32[]{:S(2)}, u32[]{:S(2)}) collective-permute-start(bf16[2,256,768]{2,1,0:T(8,128)(2,1)} %collective-permute-done.10.refs_3_), channel_id=1, source_target_pairs={{0,4},{4,8},{8,12},{1,5},{5,9},{9,13},{2,6},{6,10},{10,14},{3,7},{... | collective-permute-start | bytes 2359304 | tf_op jit(solution)/shard_map/ppermute | solution.py:188
  49.4 89.8 %collective-permute-start.12 = (bf16[2,256,768]{2,1,0:T(8,128)(2,1)}, bf16[2,256,768]{2,1,0:T(8,128)(2,1)}, u32[]{:S(2)}, u32[]{:S(2)}) collective-permute-start(bf16[2,256,768]{2,1,0:T(8,128)(2,1)} %collective-permute-done.10.refs_3_), channel_id=1, source_target_pairs={{4,0},{8,4},{12,8},{5,1},{9,5},{13,9},{6,2},{10,6},{14,10},{7,3},{... | collective-permute-start | bytes 2359304 | tf_op jit(solution)/shard_map/ppermute | solution.py:188
  118.6 15.3 %collective-permute-start.15 = (f32[6,8,256]{2,1,0:T(8,128)S(1)}, f32[6,8,256]{2,1,0:T(8,128)S(1)}, u32[]{:S(2)}, u32[]{:S(2)}) collective-permute-start(f32[6,8,256]{2,1,0:T(8,128)S(1)} %get-tuple-element.29.refs_6_), channel_id=1, source_target_pairs={{0,2},{1,3},{2,0},{3,1},{4,6},{5,7},{6,4},{7,5},{8,10},{9,11},{10,... | collective-permute-start | bytes 147464 | tf_op jit(solution)/shard_map/ppermute | solution.py:193
  121.2 43.1 %all-to-all-start = ((bf16[4,16,8,768]{3,2,0,1:T(8,128)(2,1)}), bf16[4,16,8,768]{3,2,0,1:T(8,128)(2,1)}, u32[]{:S(2)}, u32[]{:S(2)}) async-start(bf16[4,16,8,768]{3,2,0,1:T(8,128)(2,1)} %copy.19), calls=%async_computation | async-start | bytes 1572864 | tf_op jit(solution)/shard_map/all_to_all | solution.py:348
  128.5 18.2 %collective-permute-start.13 = (f32[6,8,256]{2,1,0:T(8,128)S(1)}, f32[6,8,256]{2,1,0:T(8,128)S(1)}, u32[]{:S(2)}, u32[]{:S(2)}) collective-permute-start(f32[6,8,256]{2,1,0:T(8,128)S(1)} %get-tuple-element.29.refs_6_), channel_id=1, source_target_pairs={{0,4},{4,8},{8,12},{1,5},{5,9},{9,13},{2,6},{6,10},{10,14},{3,7},{... | collective-permute-start | bytes 147464 | tf_op jit(solution)/shard_map/ppermute | solution.py:188
  131.7 17.0 %collective-permute-start.14 = (f32[6,8,256]{2,1,0:T(8,128)S(1)}, f32[6,8,256]{2,1,0:T(8,128)S(1)}, u32[]{:S(2)}, u32[]{:S(2)}) collective-permute-start(f32[6,8,256]{2,1,0:T(8,128)S(1)} %get-tuple-element.29.refs_6_), channel_id=1, source_target_pairs={{4,0},{8,4},{12,8},{5,1},{9,5},{13,9},{6,2},{10,6},{14,10},{7,3},{... | collective-permute-start | bytes 147464 | tf_op jit(solution)/shard_map/ppermute | solution.py:188
  133.9 14.8 %collective-permute-start.16 = (f32[6,8,256]{2,1,0:T(8,128)S(1)}, f32[6,8,256]{2,1,0:T(8,128)S(1)}, u32[]{:S(2)}, u32[]{:S(2)}) collective-permute-start(f32[6,8,256]{2,1,0:T(8,128)S(1)} %collective-permute-done.15.refs_9_), channel_id=1, source_target_pairs={{0,4},{4,8},{8,12},{1,5},{5,9},{9,13},{2,6},{6,10},{10,14},{3,7},{... | collective-permute-start | bytes 147464 | tf_op jit(solution)/shard_map/ppermute | solution.py:188
  137.0 12.7 %collective-permute-start.17 = (f32[6,8,256]{2,1,0:T(8,128)S(1)}, f32[6,8,256]{2,1,0:T(8,128)S(1)}, u32[]{:S(2)}, u32[]{:S(2)}) collective-permute-start(f32[6,8,256]{2,1,0:T(8,128)S(1)} %collective-permute-done.15.refs_9_), channel_id=1, source_target_pairs={{4,0},{8,4},{12,8},{5,1},{9,5},{13,9},{6,2},{10,6},{14,10},{7,3},{... | collective-permute-start | bytes 147464 | tf_op jit(solution)/shard_map/ppermute | solution.py:188
  139.2 22.7 %collective-permute-start.7 = (bf16[2,128,768]{2,1,0:T(8,128)(2,1)S(1)}, bf16[2,128,768]{2,1,0:T(8,128)(2,1)S(1)}, u32[]{:S(2)}, u32[]{:S(2)}) collective-permute-start(bf16[2,128,768]{2,1,0:T(8,128)(2,1)S(1)} %get-tuple-element.27), channel_id=1, source_target_pairs={{0,1},{1,0},{2,3},{3,2},{4,5},{5,4},{6,7},{7,6},{8,9},{9,8},{10,11... | collective-permute-start | bytes 1179656 | tf_op jit(solution)/shard_map/ppermute | solution.py:193
  160.9 2.3 %collective-permute-start.18 = (bf16[2,128,768]{2,1,0:T(8,128)(2,1)S(1)}, bf16[2,128,768]{2,1,0:T(8,128)(2,1)S(1)}, u32[]{:S(2)}, u32[]{:S(2)}) collective-permute-start(bf16[2,128,768]{2,1,0:T(8,128)(2,1)S(1)} %get-tuple-element.31), channel_id=1, source_target_pairs={{0,1},{1,0},{2,3},{3,2},{4,5},{5,4},{6,7},{7,6},{8,9},{9,8},{10,11... | collective-permute-start | bytes 1179656 | tf_op jit(solution)/shard_map/ppermute | solution.py:193
  (8 other events, 64.5 us)
where the time goes:
time: 168 us; the launch traced here: 167 us
  starting transfers between devices  49.6 us (30%)
  blocking collectives  46.1 us (27%)
  Pallas kernels  30.4 us (18%)
  waiting for transfers between devices  20.8 us (12%)
  between operations  8.92 us (5%)
  local copies, waits for them, and re-layouts  6.96 us (4%)
  other arithmetic  4.1 us (2%)
    all_gather x1, blocking collectives, per_device(): lax.all_gather(text_stats, ('wid', 'hgt'))  46.1 us
    ppermute x12, starting transfers between devices, shifted(): return lax.ppermute(value, axis, pairs)  35.1 us
    pallas_call x1, Pallas kernels, per_device(): pl.pallas_call(functools.partial(query_kernel, count), grid_spec=pltpu.Pr...  13.1 us
    ppermute x7, waiting for transfers between devices, swapped(): lax.ppermute(value, 'hgt', [(at, at ^ stride) for at in range(count)])  11.8 us
    pallas_call x1, Pallas kernels, per_device(): pl.pallas_call(functools.partial(key_kernel, count), grid_spec=pltpu.Pref...  11.2 us
    ppermute x12, waiting for transfers between devices, shifted(): return lax.ppermute(value, axis, pairs)  8.98 us
    all_to_all x1, starting transfers between devices, per_device(): landed = lax.all_to_all(packed, ('wid', 'hgt'), 1, 1)  7.38 us
    ppermute x7, starting transfers between devices, swapped(): lax.ppermute(value, 'hgt', [(at, at ^ stride) for at in range(count)])  7.08 us
  transfers between devices with their start and end apart: 20, of which 6 were waited for; matrix products, arithmetic and copies ran while one was open for 3% of the time, Pallas kernels for 18%

commit v1 on v0

v1 whole, which is shorter than its diff:
```python
import functools

import jax
import jax.numpy as jnp
from jax import lax
from jax.experimental import pallas as pl
from jax.experimental.pallas import tpu as pltpu
from jax.sharding import PartitionSpec as P

D = 128
SCALE = D ** (-0.5)
NEG = -1e30
F32 = jnp.float32
BF16 = jnp.bfloat16
def dot_nt(a, b):
    return lax.dot_general(a, b, (((1,), (1,)), ((), ())), preferred_element_type=F32)


def dot_nn(a, b):
    return lax.dot_general(a, b, (((1,), (0,)), ((), ())), preferred_element_type=F32)


def dot_tn(a, b):
    return lax.dot_general(a, b, (((0,), (0,)), ((), ())), preferred_element_type=F32)


def round_bf16(x):
    return x.astype(BF16).astype(F32)


def when(conds, run):
    conds = [c for c in conds if c is not None]
    if not conds:
        run()
        return
    total = conds[0]
    for c in conds[1:]:
        total = jnp.logical_and(total, c)
    pl.when(total)(run)


def neither(conds, run):
    conds = [c for c in conds if c is not None]
    if conds:
        total = conds[0]
        for c in conds[1:]:
            total = jnp.logical_and(total, c)
        pl.when(jnp.logical_not(total))(run)


def whole_kernel(
    wid_size,
    hgt_size,
    gate_query,
    gate_key,
    latent_key,
    latent_value,
    latent_query,
    latent_grad,
    text_query,
    text_key,
    text_value,
    text_grad,
    text_bias,
    self_bias,
    out0,
    out1,
    out2,
    out3,
    text_out,
    tiles,
    score,
    stats,
    text_stats,
    near_keys,
    self_keys,
    text_parts,
    text_landed,
    back,
    landed,
    load_sem,
    half_send,
    half_recv,
    tile_send,
    tile_recv,
    stat_send,
    stat_recv,
    text_send,
    text_recv,
    part_send,
    part_recv,
    back_send,
    back_recv,
):
    outs = (out0, out1, out2, out3)
    count = tiles.shape[1]
    size, width = tiles.shape[2], tiles.shape[3]
    half = size // 2
    heads = width // D
    text = text_query.shape[0]
    devices = wid_size * hgt_size
    tile_rows = hgt_size // 2
    tile_count = devices // 2
    grain = text_parts.shape[2]
    owned = text // devices

    wid, hgt = lax.axis_index("wid"), lax.axis_index("hgt")
    par = lax.rem(hgt, 2)
    row = hgt // 2
    rank = wid * hgt_size + hgt
    mine = pl.multiple_of(par * width, D)
    other = pl.multiple_of((1 - par) * width, D)
    tile_at = row * wid_size + wid
    mate = {"wid": wid, "hgt": hgt + 1 - 2 * par}

    def rank_peer(step):
        peer = lax.rem(rank + step, devices)
        return peer, {"wid": peer // hgt_size, "hgt": lax.rem(peer, hgt_size)}

    def tile_peer(step):
        peer = lax.rem(tile_at + step, tile_count)
        return {"wid": lax.rem(peer, wid_size), "hgt": 2 * (peer // wid_size) + par}

    def copy(src, dst, send, recv, device):
        return pltpu.make_async_remote_copy(
            src_ref=src,
            dst_ref=dst,
            send_sem=send,
            recv_sem=recv,
            device_id=device,
            device_id_type=pl.DeviceIdType.MESH,
        )

    has_left, has_right = wid > 0, wid < wid_size - 1
    left = {"wid": jnp.maximum(wid - 1, 0), "hgt": hgt}
    right = {"wid": jnp.minimum(wid + 1, wid_size - 1), "hgt": hgt}
    sides = [(1, right, has_right, has_left), (2, left, has_left, has_right)]
    if hgt_size == 4:
        uprights = [(1, {"wid": wid, "hgt": lax.rem(hgt + 2, 4)}, None, None)]
    else:
        has_up, has_down = row > 0, row < tile_rows - 1
        down = {"wid": wid, "hgt": jnp.minimum(hgt + 2, hgt_size - 2 + par)}
        up = {"wid": wid, "hgt": jnp.maximum(hgt - 2, par)}
        uprights = [(1, down, has_down, has_up), (2, up, has_up, has_down)]

    barrier = pltpu.get_barrier_semaphore()

    @pl.loop(1, devices)
    def _(step):
        _, device = rank_peer(step)
        pl.semaphore_signal(barrier, inc=1, device_id=device, device_id_type=pl.DeviceIdType.MESH)

    arrays = (latent_key, latent_value, latent_query, latent_grad)
    loads = [
        pltpu.make_async_copy(
            arrays[a].at[:, pl.ds(mine, width)], tiles.at[a, 0, pl.ds(0, half)], load_sem.at[a]
        )
        for a in range(4)
    ]
    for load in loads:
        load.start()
    pl.semaphore_wait(barrier, devices - 1)
    halves = [
        copy(
            arrays[a].at[:, pl.ds(other, width)],
            tiles.at[a, 0, pl.ds(half, half)],
            half_send.at[a],
            half_recv.at[a],
            mate,
        )
        for a in range(4)
    ]
    for move in halves:
        move.start()

    def hop(a, source, target, device):
        return copy(
            tiles.at[a, source],
            tiles.at[a, target],
            tile_send.at[a, target],
            tile_recv.at[a, target],
            device,
        )

    def stat_hop(source, target, device):
        return copy(
            stats.at[source],
            stats.at[target],
            stat_send.at[target],
            stat_recv.at[target],
            device,
        )

    sent = []

    def launch(make, conds):
        when(conds, lambda: make().start())
        sent.append((make, conds))

    def arrive(make, conds):
        when(conds, lambda: make().wait_recv())

    def first_hops(a):
        for r, device, go, _ in uprights:
            launch(functools.partial(hop, a, 0, 3 * r, device), [go])
        for c, device, go, _ in sides:
            launch(functools.partial(hop, a, 0, c, device), [go])

    def second_hops(a):
        if a != 2:
            for r, device, _, come in uprights:
                arrive(lambda: hop(a, 0, 3 * r, device), [come])
            for r, _, _, come in uprights:
                for c, device, go, _ in sides:
                    launch(functools.partial(hop, a, 3 * r, 3 * r + c, device), [go, come])
        else:
            for c, device, _, come in sides:
                arrive(lambda: hop(a, 0, c, device), [come])
            for r, device, go, _ in uprights:
                for c, _, _, come in sides:
                    launch(functools.partial(hop, a, c, 3 * r + c, device), [go, come])

    def all_arrived(a):
        if a != 2:
            for c, device, _, come in sides:
                arrive(lambda: hop(a, 0, c, device), [come])
        else:
            for r, device, _, come in uprights:
                arrive(lambda: hop(a, 0, 3 * r, device), [come])
        for r, _, _, come_row in uprights:
            for c, device, _, come in sides:
                arrive(lambda: hop(a, 0, 3 * r + c, device), [come, come_row])

    def clear(slot, conds):
        def run():
            for a in range(4):
                tiles[a, slot] = jnp.zeros((size, width), BF16)
            stats[slot] = jnp.zeros(stats.shape[1:], F32)

        neither(conds, run)

    for a in range(4):
        loads[a].wait()
        halves[a].wait_recv()
        first_hops(a)
    for c, _, _, come in sides:
        clear(c, [come])
    for r, _, _, come_row in uprights:
        clear(3 * r, [come_row])
        for c, _, _, come in sides:
            clear(3 * r + c, [come, come_row])

    def lanes(h):
        return pl.ds(pl.multiple_of(h * D, D), D)

    def text_lanes(h):
        return pl.ds(pl.multiple_of(mine + h * D, D), D)

    def text_scores(h):
        query, grad = text_query[:, text_lanes(h)], text_grad[:, text_lanes(h)]
        near = dot_nt(tiles[0, 0, :, lanes(h)], query) * SCALE
        own = dot_nt(text_key[:, text_lanes(h)], query) * SCALE + self_bias[...]
        dp_near = dot_nt(tiles[1, 0, :, lanes(h)], grad)
        dp_own = dot_nt(text_value[:, text_lanes(h)], grad)
        return query, grad, near, own, dp_near, dp_own

    @pl.loop(0, heads)
    def _(h):
        _, _, near, own, dp_near, dp_own = text_scores(h)
        top = jnp.maximum(
            jnp.max(near, axis=0, keepdims=True), jnp.max(own, axis=0, keepdims=True)
        )
        e_near = jnp.exp(near - top)
        e_own = jnp.exp(own - top)
        total = jnp.sum(e_near, axis=0, keepdims=True) + jnp.sum(e_own, axis=0, keepdims=True)
        mix = jnp.sum(e_near * dp_near, axis=0, keepdims=True) + jnp.sum(
            e_own * dp_own, axis=0, keepdims=True
        )
        text_stats[0, h] = jnp.concatenate(
            [top, total, mix, jnp.zeros((5, top.shape[1]), F32)], axis=0
        )

    def text_copy(step):
        return copy(
            text_stats.at[0],
            text_stats.at[step],
            text_send.at[step],
            text_recv.at[step],
            tile_peer(step),
        )

    @pl.loop(1, tile_count)
    def _(step):
        text_copy(step).start()

    second_hops(0)
    second_hops(1)

    @pl.loop(1, tile_count)
    def _(step):
        text_copy(step).wait_recv()

    def spread(at, h, value):
        text_parts[:, at, :, lanes(h)] = value.reshape(text // grain, grain, D).astype(BF16)

    @pl.loop(0, heads)
    def _(h):
        query, grad, near, own, dp_near, dp_own = text_scores(h)
        parts = text_stats[:, h]
        tops = parts[:, 0, :]
        top = jnp.max(tops, axis=0, keepdims=True)
        factor = jnp.exp(tops - top)
        total = jnp.sum(parts[:, 1, :] * factor, axis=0, keepdims=True)
        delta = jnp.sum(parts[:, 2, :] * factor, axis=0, keepdims=True) / total
        lse = top + jnp.log(total)
        p_near = jnp.exp(near - lse)
        p_own = jnp.exp(own - lse)
        low_near = p_near.astype(BF16)
        low_own = p_own.astype(BF16)
        ds_near = (p_near * (dp_near - delta)).astype(BF16)
        ds_own = (p_own * (dp_own - delta)).astype(BF16)
        spread(
            0,
            h,
            dot_tn(low_near, tiles[1, 0, :, lanes(h)])
            + dot_tn(low_own, text_value[:, text_lanes(h)]),
        )
        spread(
            1,
            h,
            dot_tn(ds_near, tiles[0, 0, :, lanes(h)]) + dot_tn(ds_own, text_key[:, text_lanes(h)]),
        )
        self_keys[0, :, lanes(h)] = dot_nn(ds_own, query)
        self_keys[1, :, lanes(h)] = dot_nn(low_own, grad)
        near_keys[0, :, lanes(h)] = dot_nn(ds_near, query)
        near_keys[1, :, lanes(h)] = dot_nn(low_near, grad)

    second_hops(2)
    second_hops(3)
    all_arrived(0)
    all_arrived(1)

    spans = [(at * size, size) for at in range(count)] + [(count * size, text)]

    @pl.loop(0, heads)
    def _(h):
        query, grad = tiles[2, 0, :, lanes(h)], tiles[3, 0, :, lanes(h)]

        def key_of(at):
            return tiles[0, at, :, lanes(h)] if at < count else text_key[:, text_lanes(h)]

        def value_of(at):
            return tiles[1, at, :, lanes(h)] if at < count else text_value[:, text_lanes(h)]

        top = None
        for at, (first, length) in enumerate(spans):
            part = dot_nt(key_of(at), query) * SCALE
            part = part + (gate_query[at] if at < count else text_bias[...][:, :1])
            score[first : first + length] = part
            peak = jnp.max(part, axis=0, keepdims=True)
            top = peak if top is None else jnp.maximum(top, peak)
        shift = round_bf16(top)
        total = jnp.zeros_like(shift)
        for first, length in spans:
            weight = jnp.exp(score[first : first + length] - shift)
            score[first : first + length] = weight
            total = total + jnp.sum(weight, axis=0, keepdims=True)
        inverse = round_bf16(1.0 / total)
        out = jnp.zeros((D, size), F32)
        for at, (first, length) in enumerate(spans):
            low = (score[first : first + length] * inverse).astype(BF16)
            out = out + dot_tn(value_of(at), low)
            if at == count:
                spread(3, h, self_keys[1, :, lanes(h)] + dot_nn(low, grad))
        out = round_bf16(out)
        delta = round_bf16(jnp.sum(grad.astype(F32).T * out, axis=0, keepdims=True))
        query_grad = jnp.zeros((D, size), F32)
        for at, (first, length) in enumerate(spans):
            dp = dot_nt(value_of(at), grad)
            ds = (score[first : first + length] * inverse * (dp - delta)).astype(BF16)
            query_grad = query_grad + dot_tn(key_of(at), ds)
            if at == count:
                spread(2, h, self_keys[0, :, lanes(h)] + dot_nn(ds, query))
        for at, value in enumerate((out.T, (query_grad * SCALE).T)):
            value = value.astype(BF16)
            outs[at][:, text_lanes(h)] = value[:half]
            back[at, :, lanes(h)] = value[half:]
        stats[0, h] = jnp.concatenate([shift, inverse, delta, jnp.zeros((5, size), F32)], axis=0)

    for r, device, go, _ in uprights:
        launch(functools.partial(stat_hop, 0, 3 * r, device), [go])
    for c, device, go, _ in sides:
        launch(functools.partial(stat_hop, 0, c, device), [go])

    def part_copy(step):
        peer, device = rank_peer(step)
        return copy(
            text_parts.at[peer * owned // grain],
            text_landed.at[step],
            part_send.at[step],
            part_recv.at[step],
            device,
        )

    @pl.loop(1, devices)
    def _(step):
        part_copy(step).start()

    def back_copy(at):
        return copy(back.at[at], landed.at[at], back_send.at[at], back_recv.at[at], mate)

    for at in range(2):
        back_copy(at).start()

    for r, device, _, come in uprights:
        arrive(lambda: stat_hop(0, 3 * r, device), [come])
    for r, _, _, come in uprights:
        for c, device, go, _ in sides:
            launch(functools.partial(stat_hop, 3 * r, 3 * r + c, device), [go, come])
    for c, device, _, come in sides:
        arrive(lambda: stat_hop(0, c, device), [come])
    for r, _, _, come_row in uprights:
        for c, device, _, come in sides:
            arrive(lambda: stat_hop(0, 3 * r + c, device), [come, come_row])
    all_arrived(2)
    all_arrived(3)

    @pl.loop(0, heads)
    def _(h):
        key, value = tiles[0, 0, :, lanes(h)], tiles[1, 0, :, lanes(h)]
        key_grad = near_keys[0, :, lanes(h)]
        value_grad = near_keys[1, :, lanes(h)]
        for at in range(count):
            query, grad = tiles[2, at, :, lanes(h)], tiles[3, at, :, lanes(h)]
            rows = stats[at, h]
            shift, inverse, delta = rows[0:1], rows[1:2], rows[2:3]
            prob = jnp.exp(dot_nt(key, query) * SCALE + (gate_key[at] - shift)) * inverse
            ds = (prob * (dot_nt(value, grad) - delta)).astype(BF16)
            value_grad = value_grad + dot_nn(prob.astype(BF16), grad)
            key_grad = key_grad + dot_nn(ds, query)
        for at, grads in ((2, key_grad * SCALE), (3, value_grad)):
            grads = grads.astype(BF16)
            outs[at][:, text_lanes(h)] = grads[:half]
            back[at, :, lanes(h)] = grads[half:]

    for at in range(2, 4):
        back_copy(at).start()

    @pl.loop(1, devices)
    def _(step):
        part_copy(step).wait_recv()

    own_part = text_parts[rank * owned // grain].astype(F32)

    def add_pair(step, sums):
        same = sums[0] + text_landed[2 * step].astype(F32)
        return same, sums[1] + text_landed[2 * step + 1].astype(F32)

    same, cross = lax.fori_loop(
        1, devices // 2, add_pair, (own_part, text_landed[1].astype(F32))
    )
    text_out[:, :, pl.ds(mine, width)] = same
    text_out[:, :, pl.ds(other, width)] = cross

    for at in range(4):
        back_copy(at).wait_recv()
        outs[at][:, pl.ds(other, width)] = landed[at]

    for move in halves:
        move.wait_send()
    for make, conds in sent:
        when(conds, lambda: make().wait_send())

    @pl.loop(1, tile_count)
    def _(step):
        text_copy(step).wait_send()

    @pl.loop(1, devices)
    def _(step):
        part_copy(step).wait_send()

    for at in range(4):
        back_copy(at).wait_send()


def per_device(
    latent_query,
    latent_key,
    latent_value,
    latent_grad,
    text_query,
    text_key,
    text_value,
    text_grad,
    text_valid,
    windows,
):
    block = latent_query.shape
    channels = block[3]
    rows = block[0] * block[1] * block[2]
    size = 2 * rows
    width = channels // 2
    heads = width // D
    text = text_query.shape[0]
    wid_size, hgt_size = lax.axis_size("wid"), lax.axis_size("hgt")
    devices = wid_size * hgt_size
    wid_at, hgt_at = lax.axis_index("wid"), lax.axis_index("hgt")
    tile_row, tile_rows = hgt_at // 2, hgt_size // 2
    tile_here = tile_row * wid_size + wid_at

    row_steps = [0, 1 - 2 * tile_row] if hgt_size == 4 else [0, -1, 1]
    sees, seen = [], []
    for dr in row_steps:
        for dc in (0, -1, 1):
            row, col = tile_row + dr, wid_at + dc
            inside = (row >= 0) & (row < tile_rows) & (col >= 0) & (col < wid_size)
            other = jnp.clip(row, 0, tile_rows - 1) * wid_size + jnp.clip(col, 0, wid_size - 1)
            slot = (dr + 1) * 3 + dc + 1
            sees.append(inside & (windows[tile_here, slot] >= 0))
            seen.append(inside & (windows[other, 8 - slot] >= 0))
    count = len(sees)
    gate_query = jnp.where(jnp.stack(sees), 0.0, NEG).astype(F32)
    gate_key = jnp.where(jnp.stack(seen), 0.0, NEG).astype(F32)
    text_bias = jnp.broadcast_to(
        jnp.where(text_valid == 1, 0.0, NEG).astype(F32)[:, None], (text, text)
    )
    self_bias = jnp.where(tile_here == 0, text_bias, NEG)

    owned = text // devices
    grain = max(owned, 8)
    flat = [a.reshape(rows, channels) for a in (latent_key, latent_value, latent_query, latent_grad)]
    smem = pl.BlockSpec(memory_space=pltpu.SMEM)
    hbm = pl.BlockSpec(memory_space=pl.ANY)
    vmem = pl.BlockSpec(memory_space=pltpu.VMEM)
    dma = pltpu.SemaphoreType.DMA
    results = pl.pallas_call(
        functools.partial(whole_kernel, wid_size, hgt_size),
        in_specs=[smem] * 2 + [hbm] * 4 + [vmem] * 6,
        out_specs=[vmem] * 5,
        out_shape=[jax.ShapeDtypeStruct((rows, channels), BF16)] * 4
        + [jax.ShapeDtypeStruct((4, grain, channels), F32)],
        scratch_shapes=[
            pltpu.VMEM((4, count, size, width), BF16),
            pltpu.VMEM((count * size + text, size), F32),
            pltpu.VMEM((count, heads, 8, size), F32),
            pltpu.VMEM((devices // 2, heads, 8, text), F32),
            pltpu.VMEM((2, size, width), F32),
            pltpu.VMEM((2, text, width), F32),
            pltpu.VMEM((text // grain, 4, grain, width), BF16),
            pltpu.VMEM((devices, 4, grain, width), BF16),
            pltpu.VMEM((4, rows, width), BF16),
            pltpu.VMEM((4, rows, width), BF16),
            dma((4,)),
            dma((4,)),
            dma((4,)),
            dma((4, count)),
            dma((4, count)),
            dma((count,)),
            dma((count,)),
            dma((devices // 2,)),
            dma((devices // 2,)),
            dma((devices,)),
            dma((devices,)),
            dma((4,)),
            dma((4,)),
        ],
        compiler_params=pltpu.CompilerParams(
            collective_id=0, has_side_effects=True, vmem_limit_bytes=52 * 1024 * 1024
        ),
        name="joint_attention",
    )(
        gate_query,
        gate_key,
        *flat,
        text_query,
        text_key,
        text_value,
        text_grad,
        text_bias,
        self_bias,
    )
    latent = [a.reshape(block) for a in results[:4]]
    rank = wid_at * hgt_size + hgt_at
    text_rows = lax.dynamic_slice_in_dim(results[4], rank * owned % grain, owned, 1)
    text_outs = [
        text_rows[0].astype(BF16),
        (text_rows[1] * SCALE).astype(BF16),
        (text_rows[2] * SCALE).astype(BF16),
        text_rows[3].astype(BF16),
    ]
    return tuple(latent + text_outs)


def solution(mesh):
    tiles = P("grp", "hgt", "wid", None)
    rows = P(("grp", "wid", "hgt"), None)
    return jax.shard_map(
        per_device,
        mesh=mesh,
        in_specs=(tiles,) * 4 + (P("grp", None),) * 4 + (P("grp"), P()),
        out_specs=(tiles,) * 4 + (rows,) * 4,
        check_vma=False,
    )
```

time: 168 us -> 122 us (0.73)
  Pallas kernels: 30.4 us -> 107 us
  starting transfers between devices: 49.6 us -> 0 us
  blocking collectives: 46.1 us -> 0 us
  waiting for transfers between devices: 20.8 us -> 0 us
  other arithmetic: 4.1 us -> 0.65 us
    pallas_call x6 -> x1, Pallas kernels: 30.4 us -> 107 us  [per_device(): pl.pallas_call(functools.partial(whole_kernel, wid_size, hgt_size), in_sp...]
    all_gather x1 -> x0, blocking collectives: 46.1 us -> none  [per_device(): lax.all_gather(text_stats, ('wid', 'hgt'))]
    ppermute x19 -> x0, starting transfers between devices: 42.2 us -> none  [the longest x12 35.1 us: shifted(): return lax.ppermute(value, axis, pairs)]
    ppermute x19 -> x0, waiting for transfers between devices: 20.7 us -> none  [the longest x7 11.8 us: swapped(): lax.ppermute(value, 'hgt', [(at, at ^ stride) for at in range(count)])]
    all_to_all x1 -> x0, starting transfers between devices: 7.38 us -> none  [per_device(): landed = lax.all_to_all(packed, ('wid', 'hgt'), 1, 1)]
    select_n x3 -> x0, other arithmetic: 2.13 us -> none  [the longest x2 2.13 us: halves_back(): jnp.where(parity == 0, jnp.concatenate([mine, theirs], axis=-1), jnp.conc...]
    unnamed x26 -> x8, local copies, waits for them, and re-layouts: 4.15 us -> 4.31 us
  transfers between devices with their start and end apart: 20 -> 0, of which waited for: 6 -> 0; matrix products, arithmetic and copies ran while one was open for 3% -> 0% of each run, Pallas kernels for 18% -> 0%
where the time goes in v1:
time: 122 us
  Pallas kernels  107 us (88%)
  between operations  8.53 us (7%)
  local copies, waits for them, and re-layouts  5.99 us (5%)
    pallas_call x1, Pallas kernels, per_device(): pl.pallas_call(functools.partial(whole_kernel, wid_size, hgt_size), in_sp...  107 us
    unnamed x8, local copies, waits for them, and re-layouts  4.31 us

profile of v1, /device:TPU:9, one launch (start us, length us, event | category | flops | bytes accessed | tf_op | source)
XLA Modules:
  0.0 122.0 jit_solution(5970117027224949231)
XLA Ops:
  0.8 0.0 copy-start
  0.8 0.7 copy-done
  1.4 0.7 fusion.2
  9.9 0.1 stack.55
  10.0 0.1 stack.48
  10.1 0.0 copy-start.1
  10.1 0.7 copy-done.1
  10.8 0.1 broadcast_in_dim.33.self_bias
  10.8 0.1 broadcast_in_dim.32.text_bias
  10.9 106.8 %joint_attention.1 = (bf16[128,1536]{1,0:T(8,128)(2,1)S(1)}, bf16[128,1536]{1,0:T(8,128)(2,1)S(1)}, bf16[128,1536]{1,0:T(8,128)(2,1)S(1)}, bf16[128,1536]{1,0:T(8,128)(2,1)S(1)}, f32[4,8,1536]{2,1,0:T(8,128)S(1)}) custom-call(f32[6]{0:T(128)S(1)} %get-tuple-element.37.gate_query, f32[6]{0:T(128)S(1)} %get-tuple-element.36.gate_key, ...), custom_call_target="tpu_custom_call" | custom-call | tf_op jit(solution)/shard_map/joint_attention/pallas_call | solution.py:536
  117.7 0.6 fusion.1
  118.4 0.6 slice_bitcast_fusion
  119.0 0.7 copy.22
  119.8 0.7 copy.23
  120.5 0.7 copy.24
  121.2 0.7 copy.25
  (3 shorter events, 0.0 us)
Async XLA Ops:
  0.8 0.7 copy-start
  10.1 0.7 copy-start.1

commit v2 on v1

--- a/solution.py
+++ b/solution.py
@@ -51,24 +51,23 @@
 def whole_kernel(
     wid_size,
     hgt_size,
-    gate_query,
-    gate_key,
+    windows,
     latent_key,
     latent_value,
     latent_query,
     latent_grad,
-    text_query,
-    text_key,
-    text_value,
-    text_grad,
+    text_query_all,
+    text_key_all,
+    text_value_all,
+    text_grad_all,
     text_bias,
-    self_bias,
     out0,
     out1,
     out2,
     out3,
     text_out,
     tiles,
+    text_own,
     score,
     stats,
     text_stats,
@@ -79,6 +78,7 @@
     back,
     landed,
     load_sem,
+    text_load_sem,
     half_send,
     half_recv,
     tile_send,
@@ -97,7 +97,7 @@
     size, width = tiles.shape[2], tiles.shape[3]
     half = size // 2
     heads = width // D
-    text = text_query.shape[0]
+    text = text_bias.shape[0]
     devices = wid_size * hgt_size
     tile_rows = hgt_size // 2
     tile_count = devices // 2
@@ -159,6 +159,31 @@
     ]
     for load in loads:
         load.start()
+    text_loads = [
+        pltpu.make_async_copy(
+            array.at[:, pl.ds(mine, width)], text_own.at[a], text_load_sem.at[a]
+        )
+        for a, array in enumerate((text_query_all, text_key_all, text_value_all, text_grad_all))
+    ]
+    for load in text_loads:
+        load.start()
+    text_query, text_key, text_value, text_grad = (text_own.at[a] for a in range(4))
+
+    self_gate = jnp.where(tile_at == 0, 0.0, NEG).astype(F32)
+    gate_query, gate_key = [], []
+    for dr in [0, 1 - 2 * row] if hgt_size == 4 else [0, -1, 1]:
+        for dc in (0, -1, 1):
+            near_row, near_col = row + dr, wid + dc
+            inside = (near_row >= 0) & (near_row < tile_rows)
+            inside = inside & (near_col >= 0) & (near_col < wid_size)
+            near_row = jnp.clip(near_row, 0, tile_rows - 1)
+            near_tile = near_row * wid_size + jnp.clip(near_col, 0, wid_size - 1)
+            slot = (dr + 1) * 3 + dc + 1
+            for gates, entry in (
+                (gate_query, windows[tile_at, slot]),
+                (gate_key, windows[near_tile, 8 - slot]),
+            ):
+                gates.append(jnp.where(inside & (entry >= 0), 0.0, NEG).astype(F32))
     pl.semaphore_wait(barrier, devices - 1)
     halves = [
         copy(
@@ -200,9 +225,11 @@
     def arrive(make, conds):
         when(conds, lambda: make().wait_recv())
 
-    def first_hops(a):
+    def upright_hops(a):
         for r, device, go, _ in uprights:
             launch(functools.partial(hop, a, 0, 3 * r, device), [go])
+
+    def side_hops(a):
         for c, device, go, _ in sides:
             launch(functools.partial(hop, a, 0, c, device), [go])
 
@@ -220,13 +247,15 @@
                 for c, _, _, come in sides:
                     launch(functools.partial(hop, a, c, 3 * r + c, device), [go, come])
 
-    def all_arrived(a):
+    def direct_arrived(a):
         if a != 2:
             for c, device, _, come in sides:
                 arrive(lambda: hop(a, 0, c, device), [come])
         else:
             for r, device, _, come in uprights:
                 arrive(lambda: hop(a, 0, 3 * r, device), [come])
+
+    def corners_arrived(a):
         for r, _, _, come_row in uprights:
             for c, device, _, come in sides:
                 arrive(lambda: hop(a, 0, 3 * r + c, device), [come, come_row])
@@ -242,7 +271,9 @@
     for a in range(4):
         loads[a].wait()
         halves[a].wait_recv()
-        first_hops(a)
+        if a < 2:
+            upright_hops(a)
+            side_hops(a)
     for c, _, _, come in sides:
         clear(c, [come])
     for r, _, _, come_row in uprights:
@@ -253,15 +284,18 @@
     def lanes(h):
         return pl.ds(pl.multiple_of(h * D, D), D)
 
-    def text_lanes(h):
+    for load in text_loads:
+        load.wait()
+
+    def out_lanes(h):
         return pl.ds(pl.multiple_of(mine + h * D, D), D)
 
     def text_scores(h):
-        query, grad = text_query[:, text_lanes(h)], text_grad[:, text_lanes(h)]
+        query, grad = text_query[:, lanes(h)], text_grad[:, lanes(h)]
         near = dot_nt(tiles[0, 0, :, lanes(h)], query) * SCALE
-        own = dot_nt(text_key[:, text_lanes(h)], query) * SCALE + self_bias[...]
+        own = dot_nt(text_key[:, lanes(h)], query) * SCALE + (text_bias[...] + self_gate)
         dp_near = dot_nt(tiles[1, 0, :, lanes(h)], grad)
-        dp_own = dot_nt(text_value[:, text_lanes(h)], grad)
+        dp_own = dot_nt(text_value[:, lanes(h)], grad)
         return query, grad, near, own, dp_near, dp_own
 
     @pl.loop(0, heads)
@@ -295,6 +329,8 @@
 
     second_hops(0)
     second_hops(1)
+    upright_hops(2)
+    upright_hops(3)
 
     @pl.loop(1, tile_count)
     def _(step):
@@ -323,34 +359,41 @@
             0,
             h,
             dot_tn(low_near, tiles[1, 0, :, lanes(h)])
-            + dot_tn(low_own, text_value[:, text_lanes(h)]),
+            + dot_tn(low_own, text_value[:, lanes(h)]),
         )
         spread(
             1,
             h,
-            dot_tn(ds_near, tiles[0, 0, :, lanes(h)]) + dot_tn(ds_own, text_key[:, text_lanes(h)]),
+            dot_tn(ds_near, tiles[0, 0, :, lanes(h)]) + dot_tn(ds_own, text_key[:, lanes(h)]),
         )
         self_keys[0, :, lanes(h)] = dot_nn(ds_own, query)
         self_keys[1, :, lanes(h)] = dot_nn(low_own, grad)
         near_keys[0, :, lanes(h)] = dot_nn(ds_near, query)
         near_keys[1, :, lanes(h)] = dot_nn(low_near, grad)
 
-    second_hops(2)
+    for a in range(2):
+        direct_arrived(a)
+    for a in range(2):
+        corners_arrived(a)
+    side_hops(2)
+    side_hops(3)
     second_hops(3)
-    all_arrived(0)
-    all_arrived(1)
 
     spans = [(at * size, size) for at in range(count)] + [(count * size, text)]
 
     @pl.loop(0, heads)
     def _(h):
+        @pl.when(h == heads // 2)
+        def _():
+            second_hops(2)
+
         query, grad = tiles[2, 0, :, lanes(h)], tiles[3, 0, :, lanes(h)]
 
         def key_of(at):
-            return tiles[0, at, :, lanes(h)] if at < count else text_key[:, text_lanes(h)]
+            return tiles[0, at, :, lanes(h)] if at < count else text_key[:, lanes(h)]
 
         def value_of(at):
-            return tiles[1, at, :, lanes(h)] if at < count else text_value[:, text_lanes(h)]
+            return tiles[1, at, :, lanes(h)] if at < count else text_value[:, lanes(h)]
 
         top = None
         for at, (first, length) in enumerate(spans):
@@ -383,7 +426,7 @@
                 spread(2, h, self_keys[0, :, lanes(h)] + dot_nn(ds, query))
         for at, value in enumerate((out.T, (query_grad * SCALE).T)):
             value = value.astype(BF16)
-            outs[at][:, text_lanes(h)] = value[:half]
+            outs[at][:, out_lanes(h)] = value[:half]
             back[at, :, lanes(h)] = value[half:]
         stats[0, h] = jnp.concatenate([shift, inverse, delta, jnp.zeros((5, size), F32)], axis=0)
 
@@ -419,18 +462,14 @@
             launch(functools.partial(stat_hop, 3 * r, 3 * r + c, device), [go, come])
     for c, device, _, come in sides:
         arrive(lambda: stat_hop(0, c, device), [come])
-    for r, _, _, come_row in uprights:
-        for c, device, _, come in sides:
-            arrive(lambda: stat_hop(0, 3 * r + c, device), [come, come_row])
-    all_arrived(2)
-    all_arrived(3)
-
-    @pl.loop(0, heads)
-    def _(h):
+    direct_arrived(2)
+    direct_arrived(3)
+
+    def key_part(h, slots):
         key, value = tiles[0, 0, :, lanes(h)], tiles[1, 0, :, lanes(h)]
         key_grad = near_keys[0, :, lanes(h)]
         value_grad = near_keys[1, :, lanes(h)]
-        for at in range(count):
+        for at in slots:
             query, grad = tiles[2, at, :, lanes(h)], tiles[3, at, :, lanes(h)]
             rows = stats[at, h]
             shift, inverse, delta = rows[0:1], rows[1:2], rows[2:3]
@@ -438,9 +477,28 @@
             ds = (prob * (dot_nt(value, grad) - delta)).astype(BF16)
             value_grad = value_grad + dot_nn(prob.astype(BF16), grad)
             key_grad = key_grad + dot_nn(ds, query)
+        return key_grad, value_grad
+
+    corners = [3 * r + c for r, _, _, _ in uprights for c in (1, 2)]
+
+    @pl.loop(0, heads)
+    def _(h):
+        key_grad, value_grad = key_part(h, [at for at in range(count) if at not in corners])
+        near_keys[0, :, lanes(h)] = key_grad
+        near_keys[1, :, lanes(h)] = value_grad
+
+    for r, _, _, come_row in uprights:
+        for c, device, _, come in sides:
+            arrive(lambda: stat_hop(0, 3 * r + c, device), [come, come_row])
+    corners_arrived(2)
+    corners_arrived(3)
+
+    @pl.loop(0, heads)
+    def _(h):
+        key_grad, value_grad = key_part(h, corners)
         for at, grads in ((2, key_grad * SCALE), (3, value_grad)):
             grads = grads.astype(BF16)
-            outs[at][:, text_lanes(h)] = grads[:half]
+            outs[at][:, out_lanes(h)] = grads[:half]
             back[at, :, lanes(h)] = grads[half:]
 
     for at in range(2, 4):
@@ -481,6 +539,21 @@
 
     for at in range(4):
         back_copy(at).wait_send()
+
+
+def finish_kernel(owned, grain, hgt_size, *refs):
+    ins, text_sums = refs[:4], refs[4]
+    outs, text_outs, sems = refs[5:9], refs[9:13], refs[13]
+    moves = [pltpu.make_async_copy(ins[a], outs[a], sems.at[a]) for a in range(4)]
+    for move in moves:
+        move.start()
+    rank = lax.axis_index("wid") * hgt_size + lax.axis_index("hgt")
+    first = 0 if owned == grain else lax.rem(rank * owned, grain)
+    for a in range(4):
+        sums = text_sums[a, pl.ds(first, owned), :]
+        text_outs[a][...] = (sums * SCALE if a in (1, 2) else sums).astype(BF16)
+    for move in moves:
+        move.wait()
 
 
 def per_device(
@@ -504,28 +577,10 @@
     text = text_query.shape[0]
     wid_size, hgt_size = lax.axis_size("wid"), lax.axis_size("hgt")
     devices = wid_size * hgt_size
-    wid_at, hgt_at = lax.axis_index("wid"), lax.axis_index("hgt")
-    tile_row, tile_rows = hgt_at // 2, hgt_size // 2
-    tile_here = tile_row * wid_size + wid_at
-
-    row_steps = [0, 1 - 2 * tile_row] if hgt_size == 4 else [0, -1, 1]
-    sees, seen = [], []
-    for dr in row_steps:
-        for dc in (0, -1, 1):
-            row, col = tile_row + dr, wid_at + dc
-            inside = (row >= 0) & (row < tile_rows) & (col >= 0) & (col < wid_size)
-            other = jnp.clip(row, 0, tile_rows - 1) * wid_size + jnp.clip(col, 0, wid_size - 1)
-            slot = (dr + 1) * 3 + dc + 1
-            sees.append(inside & (windows[tile_here, slot] >= 0))
-            seen.append(inside & (windows[other, 8 - slot] >= 0))
-    count = len(sees)
-    gate_query = jnp.where(jnp.stack(sees), 0.0, NEG).astype(F32)
-    gate_key = jnp.where(jnp.stack(seen), 0.0, NEG).astype(F32)
+    count = 6 if hgt_size == 4 else 9
     text_bias = jnp.broadcast_to(
         jnp.where(text_valid == 1, 0.0, NEG).astype(F32)[:, None], (text, text)
     )
-    self_bias = jnp.where(tile_here == 0, text_bias, NEG)
-
     owned = text // devices
     grain = max(owned, 8)
     flat = [a.reshape(rows, channels) for a in (latent_key, latent_value, latent_query, latent_grad)]
@@ -533,14 +588,15 @@
     hbm = pl.BlockSpec(memory_space=pl.ANY)
     vmem = pl.BlockSpec(memory_space=pltpu.VMEM)
     dma = pltpu.SemaphoreType.DMA
+    whole = jax.ShapeDtypeStruct((rows, channels), BF16)
     results = pl.pallas_call(
         functools.partial(whole_kernel, wid_size, hgt_size),
-        in_specs=[smem] * 2 + [hbm] * 4 + [vmem] * 6,
+        in_specs=[smem] + [hbm] * 8 + [vmem],
         out_specs=[vmem] * 5,
-        out_shape=[jax.ShapeDtypeStruct((rows, channels), BF16)] * 4
-        + [jax.ShapeDtypeStruct((4, grain, channels), F32)],
+        out_shape=[whole] * 4 + [jax.ShapeDtypeStruct((4, grain, channels), F32)],
         scratch_shapes=[
             pltpu.VMEM((4, count, size, width), BF16),
+            pltpu.VMEM((4, text, width), BF16),
             pltpu.VMEM((count * size + text, size), F32),
             pltpu.VMEM((count, heads, 8, size), F32),
             pltpu.VMEM((devices // 2, heads, 8, text), F32),
@@ -550,6 +606,7 @@
             pltpu.VMEM((devices, 4, grain, width), BF16),
             pltpu.VMEM((4, rows, width), BF16),
             pltpu.VMEM((4, rows, width), BF16),
+            dma((4,)),
             dma((4,)),
             dma((4,)),
             dma((4,)),
@@ -565,30 +622,19 @@
             dma((4,)),
         ],
         compiler_params=pltpu.CompilerParams(
-            collective_id=0, has_side_effects=True, vmem_limit_bytes=52 * 1024 * 1024
+            collective_id=0, has_side_effects=True, vmem_limit_bytes=56 * 1024 * 1024
         ),
         name="joint_attention",
-    )(
-        gate_query,
-        gate_key,
-        *flat,
-        text_query,
-        text_key,
-        text_value,
-        text_grad,
-        text_bias,
-        self_bias,
-    )
-    latent = [a.reshape(block) for a in results[:4]]
-    rank = wid_at * hgt_size + hgt_at
-    text_rows = lax.dynamic_slice_in_dim(results[4], rank * owned % grain, owned, 1)
-    text_outs = [
-        text_rows[0].astype(BF16),
-        (text_rows[1] * SCALE).astype(BF16),
-        (text_rows[2] * SCALE).astype(BF16),
-        text_rows[3].astype(BF16),
-    ]
-    return tuple(latent + text_outs)
+    )(windows, *flat, text_query, text_key, text_value, text_grad, text_bias)
+    finished = pl.pallas_call(
+        functools.partial(finish_kernel, owned, grain, hgt_size),
+        in_specs=[hbm] * 4 + [vmem],
+        out_specs=[hbm] * 4 + [vmem] * 4,
+        out_shape=[whole] * 4 + [jax.ShapeDtypeStruct((owned, channels), BF16)] * 4,
+        scratch_shapes=[dma((4,))],
+        name="finish",
+    )(*results)
+    return tuple([a.reshape(block) for a in finished[:4]] + list(finished[4:]))
 
 
 def solution(mesh):

time: 122 us -> 153 us (1.25)
  Pallas kernels: 107 us -> 150 us
  between operations: 8.53 us -> 0.65 us
  local copies, waits for them, and re-layouts: 5.99 us -> 1.36 us
    pallas_call x0 -> x1, Pallas kernels: none -> 50.3 us  [per_device(): pl.pallas_call(functools.partial(finish_kernel, owned, grain, hgt_size),...]
    pallas_call x1, Pallas kernels: 107 us -> 100 us  [per_device(): pl.pallas_call(functools.partial(whole_kernel, wid_size, hgt_size), in_sp...]
    unnamed x8 -> x2, local copies, waits for them, and re-layouts: 4.31 us -> 0.65 us
where the time goes in v2:
time: 153 us; the launch traced here: 152 us
  Pallas kernels  150 us (98%)
    pallas_call x1, Pallas kernels, per_device(): pl.pallas_call(functools.partial(whole_kernel, wid_size, hgt_size), in_sp...  100 us
    pallas_call x1, Pallas kernels, per_device(): pl.pallas_call(functools.partial(finish_kernel, owned, grain, hgt_size),...  50.3 us

profile of v2, /device:TPU:9, one launch (start us, length us, event | category | flops | bytes accessed | tf_op | source)
XLA Modules:
  0.0 152.3 jit_solution(17948800930670622009)
XLA Ops:
  0.6 0.0 copy-start
  0.6 0.6 copy-done
  1.3 0.7 broadcast_in_dim.16.text_bias
  2.0 100.0 %joint_attention.1 = (bf16[128,1536]{1,0:T(8,128)(2,1)}, bf16[128,1536]{1,0:T(8,128)(2,1)}, bf16[128,1536]{1,0:T(8,128)(2,1)}, bf16[128,1536]{1,0:T(8,128)(2,1)}, f32[4,8,1536]{2,1,0:T(8,128)}) custom-call(s32[8,9]{1,0:T(8,128)} %windows.1, bf16[128,1536]{1,0:T(8,128)(2,1)} %bitcast.8, bf16[128,1536]{1,0:T(8,128)(2,1)} %bitcast.9, ...), custom_call_target="tpu_custom_call" | custom-call | tf_op jit(solution)/shard_map/joint_attention/pallas_call | solution.py:592
  102.0 50.3 %finish.1 = (bf16[128,1536]{1,0:T(8,128)(2,1)}, bf16[128,1536]{1,0:T(8,128)(2,1)}, bf16[128,1536]{1,0:T(8,128)(2,1)}, bf16[128,1536]{1,0:T(8,128)(2,1)}, bf16[8,...) custom-call(bf16[128,1536]{1,0:T(8,128)(2,1)} %get-tuple-element.21.refs_0_, ...), custom_call_target="tpu_custom_call" | custom-call | tf_op jit(solution)/shard_map/finish/pallas_call | solution.py:629
  (1 shorter events, 0.0 us)
Async XLA Ops:
  0.6 0.7 copy-start

commit v3 on v2

--- a/solution.py
+++ b/solution.py
@@ -233,27 +233,36 @@
         for c, device, go, _ in sides:
             launch(functools.partial(hop, a, 0, c, device), [go])
 
+    def routes(a):
+        if a == 1:
+            return [(True, par == 0), (False, par == 1)]
+        return [(a == 2, None)]
+
     def second_hops(a):
-        if a != 2:
-            for r, device, _, come in uprights:
-                arrive(lambda: hop(a, 0, 3 * r, device), [come])
-            for r, _, _, come in uprights:
-                for c, device, go, _ in sides:
-                    launch(functools.partial(hop, a, 3 * r, 3 * r + c, device), [go, come])
-        else:
-            for c, device, _, come in sides:
-                arrive(lambda: hop(a, 0, c, device), [come])
-            for r, device, go, _ in uprights:
-                for c, _, _, come in sides:
-                    launch(functools.partial(hop, a, c, 3 * r + c, device), [go, come])
+        for by_side_first, use in routes(a):
+            if by_side_first:
+                for c, device, _, come in sides:
+                    arrive(functools.partial(hop, a, 0, c, device), [come, use])
+                for r, device, go, _ in uprights:
+                    for c, _, _, come in sides:
+                        launch(functools.partial(hop, a, c, 3 * r + c, device), [go, come, use])
+            else:
+                for r, device, _, come in uprights:
+                    arrive(functools.partial(hop, a, 0, 3 * r, device), [come, use])
+                for r, _, _, come in uprights:
+                    for c, device, go, _ in sides:
+                        launch(
+                            functools.partial(hop, a, 3 * r, 3 * r + c, device), [go, come, use]
+                        )
 
     def direct_arrived(a):
-        if a != 2:
-            for c, device, _, come in sides:
-                arrive(lambda: hop(a, 0, c, device), [come])
-        else:
-            for r, device, _, come in uprights:
-                arrive(lambda: hop(a, 0, 3 * r, device), [come])
+        for by_side_first, use in routes(a):
+            if by_side_first:
+                for r, device, _, come in uprights:
+                    arrive(functools.partial(hop, a, 0, 3 * r, device), [come, use])
+            else:
+                for c, device, _, come in sides:
+                    arrive(functools.partial(hop, a, 0, c, device), [come, use])
 
     def corners_arrived(a):
         for r, _, _, come_row in uprights:
@@ -543,17 +552,14 @@
 
 def finish_kernel(owned, grain, hgt_size, *refs):
     ins, text_sums = refs[:4], refs[4]
-    outs, text_outs, sems = refs[5:9], refs[9:13], refs[13]
-    moves = [pltpu.make_async_copy(ins[a], outs[a], sems.at[a]) for a in range(4)]
-    for move in moves:
-        move.start()
+    outs, text_outs = refs[5:9], refs[9:13]
+    for a in range(4):
+        outs[a][...] = ins[a][...]
     rank = lax.axis_index("wid") * hgt_size + lax.axis_index("hgt")
     first = 0 if owned == grain else lax.rem(rank * owned, grain)
     for a in range(4):
         sums = text_sums[a, pl.ds(first, owned), :]
         text_outs[a][...] = (sums * SCALE if a in (1, 2) else sums).astype(BF16)
-    for move in moves:
-        move.wait()
 
 
 def per_device(
@@ -628,10 +634,9 @@
     )(windows, *flat, text_query, text_key, text_value, text_grad, text_bias)
     finished = pl.pallas_call(
         functools.partial(finish_kernel, owned, grain, hgt_size),
-        in_specs=[hbm] * 4 + [vmem],
-        out_specs=[hbm] * 4 + [vmem] * 4,
+        in_specs=[vmem] * 5,
+        out_specs=[vmem] * 8,
         out_shape=[whole] * 4 + [jax.ShapeDtypeStruct((owned, channels), BF16)] * 4,
-        scratch_shapes=[dma((4,))],
         name="finish",
     )(*results)
     return tuple([a.reshape(block) for a in finished[:4]] + list(finished[4:]))

time: 153 us -> 101 us (0.66)
  Pallas kernels: 150 us -> 98.6 us
    pallas_call x1, Pallas kernels: 50.3 us -> 2.58 us  [per_device(): pl.pallas_call(functools.partial(finish_kernel, owned, grain, hgt_size),...]
    pallas_call x1, Pallas kernels: 100 us -> 96.1 us  [per_device(): pl.pallas_call(functools.partial(whole_kernel, wid_size, hgt_size), in_sp...]
where the time goes in v3:
time: 101 us
  Pallas kernels  98.6 us (98%)
  local copies, waits for them, and re-layouts  1.36 us (1%)
    pallas_call x1, Pallas kernels, per_device(): pl.pallas_call(functools.partial(whole_kernel, wid_size, hgt_size), in_sp...  96.1 us
    pallas_call x1, Pallas kernels, per_device(): pl.pallas_call(functools.partial(finish_kernel, owned, grain, hgt_size),...  2.58 us

profile of v3, /device:TPU:9, one launch (start us, length us, event | category | flops | bytes accessed | tf_op | source)
XLA Modules:
  0.0 100.7 jit_solution(17946717898865300832)
XLA Ops:
  0.6 0.0 copy-start
  0.6 0.6 copy-done
  1.3 0.7 broadcast_in_dim.16.text_bias
  2.0 96.1 %joint_attention.1 = (bf16[128,1536]{1,0:T(8,128)(2,1)}, bf16[128,1536]{1,0:T(8,128)(2,1)}, bf16[128,1536]{1,0:T(8,128)(2,1)}, bf16[128,1536]{1,0:T(8,128)(2,1)}, f32[4,8,1536]{2,1,0:T(8,128)}) custom-call(s32[8,9]{1,0:T(8,128)} %windows.1, bf16[128,1536]{1,0:T(8,128)(2,1)} %bitcast.8, bf16[128,1536]{1,0:T(8,128)(2,1)} %bitcast.9, ...), custom_call_target="tpu_custom_call" | custom-call | tf_op jit(solution)/shard_map/joint_attention/pallas_call | solution.py:598
  98.1 2.6 %finish.1 = (bf16[128,1536]{1,0:T(8,128)(2,1)}, bf16[128,1536]{1,0:T(8,128)(2,1)}, bf16[128,1536]{1,0:T(8,128)(2,1)}, bf16[128,1536]{1,0:T(8,128)(2,1)}, bf16[8,...) custom-call(bf16[128,1536]{1,0:T(8,128)(2,1)} %get-tuple-element.21.refs_0_, ...), custom_call_target="tpu_custom_call" | custom-call | tf_op jit(solution)/shard_map/finish/pallas_call | solution.py:635
  (1 shorter events, 0.0 us)
Async XLA Ops:
  0.6 0.7 copy-start

commit v4 on v3

--- a/solution.py
+++ b/solution.py
@@ -339,6 +339,7 @@
     second_hops(0)
     second_hops(1)
     upright_hops(2)
+    side_hops(2)
     upright_hops(3)
 
     @pl.loop(1, tile_count)
@@ -384,7 +385,6 @@
         direct_arrived(a)
     for a in range(2):
         corners_arrived(a)
-    side_hops(2)
     side_hops(3)
     second_hops(3)
 

time: 101 us -> 98.7 us (0.977)
  Pallas kernels: 98.6 us -> 95.6 us
    pallas_call x1, Pallas kernels: 96.1 us -> 93 us  [per_device(): pl.pallas_call(functools.partial(whole_kernel, wid_size, hgt_size), in_sp...]
where the time goes in v4:
time: 98.7 us; the launch traced here: 97.6 us
  Pallas kernels  95.6 us (97%)
  local copies, waits for them, and re-layouts  1.36 us (1%)
    pallas_call x1, Pallas kernels, per_device(): pl.pallas_call(functools.partial(whole_kernel, wid_size, hgt_size), in_sp...  93 us
    pallas_call x1, Pallas kernels, per_device(): pl.pallas_call(functools.partial(finish_kernel, owned, grain, hgt_size),...  2.58 us

profile of v4, /device:TPU:9, one launch (start us, length us, event | category | flops | bytes accessed | tf_op | source)
XLA Modules:
  0.0 97.6 jit_solution(13626278544549552388)
XLA Ops:
  0.6 0.0 copy-start
  0.6 0.6 copy-done
  1.3 0.7 broadcast_in_dim.16.text_bias
  2.0 93.0 %joint_attention.1 = (bf16[128,1536]{1,0:T(8,128)(2,1)}, bf16[128,1536]{1,0:T(8,128)(2,1)}, bf16[128,1536]{1,0:T(8,128)(2,1)}, bf16[128,1536]{1,0:T(8,128)(2,1)}, f32[4,8,1536]{2,1,0:T(8,128)}) custom-call(s32[8,9]{1,0:T(8,128)} %windows.1, bf16[128,1536]{1,0:T(8,128)(2,1)} %bitcast.8, bf16[128,1536]{1,0:T(8,128)(2,1)} %bitcast.9, ...), custom_call_target="tpu_custom_call" | custom-call | tf_op jit(solution)/shard_map/joint_attention/pallas_call | solution.py:598
  95.0 2.6 %finish.1 = (bf16[128,1536]{1,0:T(8,128)(2,1)}, bf16[128,1536]{1,0:T(8,128)(2,1)}, bf16[128,1536]{1,0:T(8,128)(2,1)}, bf16[128,1536]{1,0:T(8,128)(2,1)}, bf16[8,...) custom-call(bf16[128,1536]{1,0:T(8,128)(2,1)} %get-tuple-element.21.refs_0_, ...), custom_call_target="tpu_custom_call" | custom-call | tf_op jit(solution)/shard_map/finish/pallas_call | solution.py:635
  (1 shorter events, 0.0 us)
Async XLA Ops:
  0.6 0.7 copy-start
